TPU v7x, 256 devices: a whole 4x4x8 slice. The times are simulated.
256 devices in a mesh: grp: 4 (over y), lev: 64 (over x, z, core).
Axes of the slice: x: 4, y: 4, z: 8, core: 2. Of those that a mesh axis runs over, the one named last changes fastest.
Arguments:
- up_tiles: bfloat16 [512, 24, 128, 128], P(('grp', 'lev')), may hold values from -0.3125 to 0.3125
- up_at: int32 [512, 24], P(('grp', 'lev')), may hold values from 0 to 63, as said below
- down_tiles: bfloat16 [512, 24, 128, 128], P(('grp', 'lev')), may hold values from -0.3125 to 0.3125
- down_at: int32 [512, 24], P(('grp', 'lev')), may hold values from 0 to 63, as said below
- diag_tiles: bfloat16 [256, 24, 128, 128], P(('grp', 'lev')), may hold values from -6 to 6
- diag_at: int32 [256, 24], P(('grp', 'lev')), may hold values from 0 to 63, as said below
- odd_inverse: bfloat16 [256, 1024, 1024], P(('grp', 'lev')), may hold values from -6 to 6
Outputs:
- new_diag: bfloat16 [256, 1024, 1024], P(('grp', 'lev'))
- new_up: bfloat16 [256, 1024, 1024], P(('grp', 'lev'))
- new_down: bfloat16 [256, 1024, 1024], P(('grp', 'lev'))
- partial_sums: float32 [256, 1024], P(('grp', 'lev'))
Inputs may be any that keep to these rules, and one draw needn't show every extreme that they name: `up_at`: within one row the 24 tile positions are distinct. `down_at`: within one row the 24 tile positions are distinct. `diag_at`: within one row the 24 tile positions are distinct.
All inputs are finite; a program needn't handle non-finite values.
Results may differ from a plain program's by a relative error of at most 0.007.
Values may be sent and summed in bfloat16 or wider, within the bound.
A program may use at most 128 MiB of HBM per device.

v0:
```python
import jax
import jax.numpy as jnp
from jax import lax
from jax.sharding import PartitionSpec as P

TILE = 128
NT = 8
P_SIZE = 1024


def passed_along(block, axis, distance):
    devices = range(lax.axis_size(axis))
    route = [(i - distance, i) for i in devices if i - distance in devices]
    return lax.ppermute(block, axis, route)


def carried_in(value, axis, join, neutral):
    count, mine = (lax.axis_size(axis), lax.axis_index(axis))
    pieces = lax.all_gather(value, axis)
    so_far = jnp.full_like(value, 0) + jnp.asarray(neutral, value.dtype)

    def turn(position, so_far):
        longer = join(so_far, pieces[position])
        return jnp.where(position < mine, longer, so_far)

    return lax.fori_loop(0, count - 1, turn, so_far)


def expand_tiles(tiles, places):
    onehot = (places[None, :] == jnp.arange(NT * NT, dtype=jnp.int32)[:, None]).astype(jnp.bfloat16)
    blocks = jnp.einsum("pk,kij->pij", onehot, tiles, preferred_element_type=jnp.float32).astype(
        jnp.bfloat16
    )
    return blocks.reshape(NT, NT, TILE, TILE).transpose(0, 2, 1, 3).reshape(P_SIZE, P_SIZE)


def odd_products(inverse, up_block, up_places, down_block, down_places):
    first = jnp.dot(inverse, expand_tiles(up_block, up_places), preferred_element_type=jnp.float32)
    second = jnp.dot(
        inverse, expand_tiles(down_block, down_places), preferred_element_type=jnp.float32
    )
    return jnp.stack([first, second]).astype(jnp.bfloat16)


def add_terms(earlier, later):
    return earlier + later


def local(up_tiles, up_at, down_tiles, down_at, diag_tiles, diag_at, odd_inverse):
    own = odd_products(odd_inverse[0], up_tiles[1], up_at[1], down_tiles[1], down_at[1])
    below = passed_along(own, ("grp", "lev"), 1)
    even_up = expand_tiles(up_tiles[0], up_at[0])
    even_down = expand_tiles(down_tiles[0], down_at[0])
    up_low = jnp.dot(even_up, own[0], preferred_element_type=jnp.float32)
    up_high = jnp.dot(even_up, own[1], preferred_element_type=jnp.float32)
    below_low = jnp.dot(even_down, below[0], preferred_element_type=jnp.float32)
    below_high = jnp.dot(even_down, below[1], preferred_element_type=jnp.float32)
    new_up = (-up_low).astype(jnp.bfloat16)
    new_down = (-below_high).astype(jnp.bfloat16)
    diagonal = expand_tiles(diag_tiles[0], diag_at[0]).astype(jnp.float32)
    new_diag = (diagonal - up_high - below_low).astype(jnp.bfloat16)
    level = lax.axis_index(("grp", "lev"))
    count = lax.axis_size(("grp", "lev"))
    weight = (count + 2 * level).astype(jnp.float32) / count
    term = weight * jnp.mean(new_up.astype(jnp.float32), axis=0)
    zeros = jnp.zeros_like(term)
    earlier = carried_in(term, ("grp", "lev"), add_terms, zeros)
    inclusive = earlier + term
    return (new_diag[None], new_up[None], new_down[None], inclusive[None])


def solution(mesh):
    return jax.shard_map(
        local,
        mesh=mesh,
        in_specs=(
            P(("grp", "lev"), None, None, None),
            P(("grp", "lev"), None),
            P(("grp", "lev"), None, None, None),
            P(("grp", "lev"), None),
            P(("grp", "lev"), None, None, None),
            P(("grp", "lev"), None),
            P(("grp", "lev"), None, None),
        ),
        out_specs=(
            P(("grp", "lev"), None, None),
            P(("grp", "lev"), None, None),
            P(("grp", "lev"), None, None),
            P(("grp", "lev"), None),
        ),
        check_vma=False,
    )
```

profile of v0, /device:TPU:8, one launch (start us, length us, event | category | flops | bytes accessed | tf_op | source)
XLA Modules:
  0.0 164.0 jit_solution(6533590592842845328)
XLA Ops:
  7.2 0.0 copy-start
  7.2 0.0 copy-start.10
  7.2 0.0 all-gather.3.cloned.1.call-start
  7.2 1.6 fusion.53
  8.9 0.0 copy-done.10
  8.9 0.9 convert_bitcast_fusion.1
  9.8 1.7 %copy.36 = bf16[8,8,128,128]{3,1,2,0:T(8,128)(2,1)} copy(bf16[8,8,128,128]{3,1,0,2:T(8,128)(2,1)S(1)} %convert_bitcast_fusion.1) | data formatting | bytes 4194304 | tf_op jit(solution)/shard_map/reshape | solution.py:34
  11.5 0.9 convert_bitcast_fusion.4
  12.5 1.7 %copy.30 = bf16[8,8,128,128]{3,1,2,0:T(8,128)(2,1)} copy(bf16[8,8,128,128]{3,1,0,2:T(8,128)(2,1)S(1)} %convert_bitcast_fusion.4) | data formatting | bytes 4194304 | tf_op jit(solution)/shard_map/reshape | solution.py:34
  14.2 0.0 copy-done
  14.2 0.0 copy-start.2
  14.2 4.1 %fusion.22 = bf16[1024,1024]{1,0:T(8,128)(2,1)S(1)} fusion(bf16[1,1024,1024]{2,1,0:T(8,128)(2,1)S(1)} %copy-done, bf16[128,8,8,128]{3,2,1,0:T(8,128)(2,1)} %bitcast.139), kind=kOutput, calls=%fused_computation.32 | convolution fusion | flops 2148532224 | bytes 6291456 | tf_op jit(solution)/shard_map/dot_general | solution.py:38
  18.3 0.0 copy-start.5
  18.3 1.3 copy-done.5
  19.6 0.0 copy-done.2
  19.6 3.7 %convert_reduce_fusion = (f32[1024]{0:T(1024)S(1)}, bf16[1024,1024]{1,0:T(8,128)(2,1)}) fusion(bf16[1024,1024]{1,0:T(8,128)(2,1)S(1)} %fusion.22, bf16[128,8,8,128]{3,2,1,0:T(8,128)(2,1)S(1)} %bitcast.135), kind=kOutput, calls=%fused_computation.7 | convolution fusion | flops 2151676928 | bytes 6295552 | tf_op jit(solution)/shard_map/dot_general | solution.py:54
  23.3 0.0 copy-start.11
  23.3 0.6 broadcast_multiply_fusion
  23.9 0.0 all-gather.3.cloned.1.call-update
  23.9 1.5 fusion.52
  25.5 0.0 copy-done.11
  25.5 0.9 convert_bitcast_fusion.3
  26.4 0.4 copy.32
  26.8 0.0 copy-start.6
  26.8 2.4 %fusion.17 = bf16[1024,1024]{1,0:T(8,128)(2,1)S(1)} fusion(bf16[1,1024,1024]{2,1,0:T(8,128)(2,1)S(1)} %copy-done, bf16[128,8,8,128]{3,2,1,0:T(8,128)(2,1)S(1)} %bitcast.140), kind=kOutput, calls=%fused_computation.31 | convolution fusion | flops 2148532224 | bytes 6291456 | tf_op jit(solution)/shard_map/dot_general | solution.py:39
  29.2 0.0 copy-start.7
  29.2 0.0 copy-done.6
  29.2 2.6 %pad_maximum_fusion = bf16[2,1024,1024]{1,2,0:T(8,128)(2,1)} fusion(bf16[1,1024,1024]{1,2,0:T(8,128)(2,1)S(1)} %bitcast.142, bf16[1,1024,1024]{1,2,0:T(8,128)(2,1)S(1)} %bitcast.141), kind=kLoop, calls=%fused_computation.5 | loop fusion | flops 2097152 | bytes 8388608 | tf_op jit(solution)/shard_map/stack | solution.py:42
  31.8 0.1 copy-done.7
  31.9 2.1 %collective-permute-start = (bf16[2,1024,1024]{1,2,0:T(8,128)(2,1)}, bf16[2,1024,1024]{1,2,0:T(8,128)(2,1)}, u32[]{:S(2)}, u32[]{:S(2)}) collective-permute-start(bf16[2,1024,1024]{1,2,0:T(8,128)(2,1)} %pad_maximum_fusion), channel_id=1, source_target_pairs={{0,1},{1,2},{2,3},{3,4},{4,5},{5,6},{6,7},{7,8},{8,9},{9,10},{10,1... | collective-permute-start | bytes 12582920 | tf_op jit(solution)/shard_map/ppermute | solution.py:14
  34.0 0.9 convert_bitcast_fusion.2
  34.9 0.0 copy-start.9
  34.9 0.0 copy-start.12
  35.0 1.7 %copy.34 = bf16[8,8,128,128]{3,1,2,0:T(8,128)(2,1)} copy(bf16[8,8,128,128]{3,1,0,2:T(8,128)(2,1)S(1)} %convert_bitcast_fusion.2) | data formatting | bytes 4194304 | tf_op jit(solution)/shard_map/reshape | solution.py:34
  36.7 0.0 copy-done.9
  36.7 0.0 copy-done.12
  36.7 0.8 convert_bitcast_fusion
  37.5 0.0 copy-start.3
  37.5 0.0 copy-start.8
  37.6 2.4 %copy.28 = f32[8,128,8,128]{3,2,1,0:T(8,128)} copy(f32[8,128,8,128]{3,2,0,1:T(8,128)S(1)} %convert_bitcast_fusion) | data formatting | bytes 8388608 | tf_op jit(solution)/shard_map/convert_element_type | solution.py:60
  40.0 0.0 copy-done.3
  40.0 1.3 copy-done.8
  41.3 4.3 %fusion.13 = f32[1024,1024]{1,0:T(8,128)} fusion(bf16[1024,1024]{1,0:T(8,128)(2,1)S(1)} %copy-done.8, bf16[128,8,8,128]{3,2,1,0:T(8,128)(2,1)S(1)} %bitcast.136), kind=kOutput, calls=%fused_computation.21 | convolution fusion | flops 2147483648 | bytes 8388608 | tf_op jit(solution)/shard_map/dot_general | solution.py:55
  45.6 84.0 %all-gather.3.cloned.1.call-done = f32[262144]{0:T(1024)} async-done(((f32[1024]{0:T(1024)}), f32[262144]{0:T(1024)}) %all-gather.3.cloned.1.call-update) | async-done | bytes 1048592 | tf_op jit(solution)/shard_map/all_gather | solution.py:19
  129.6 1.4 reshape.59
  131.0 13.8 %while.14 = (s32[]{:T(128)}, f32[1024]{0:T(1024)S(1)}, s32[]{:T(128)}, f32[256,1024]{1,0:T(8,128)S(1)}, s32[]{:T(128)}, /*index=5*/s32[]{:T(128)}) while((s32[]{:T(128)}, f32[1024]{0:T(1024)S(1)}, s32[]{:T(128)}, f32[256,1024]{1,0:T(8,128)S(1)}, s32[]{:T(128)}, /*index=5*/s32[]{:T(128)}) %tuple.41), condition=%wide.region_2.3_spmd.clone, body=%wide.region_1.2_spmd.clone.sunk | while | flops 3076 | bytes 20573 | solution.py:26
  144.8 0.6 fusion.56
  145.4 0.0 collective-permute-done
  145.4 0.0 copy-start.1
  145.4 0.0 copy-start.4
  145.4 0.0 copy-start.13
  145.4 6.1 %fusion.31 = bf16[1,1024,1024]{2,1,0:T(8,128)(2,1)} fusion(bf16[2,1024,1024]{1,2,0:T(8,128)(2,1)} %collective-permute-done, bf16[128,8,8,128]{3,2,1,0:T(8,128)(2,1)} %bitcast.137), kind=kOutput, calls=%fused_computation.37 | convolution fusion | flops 2149580800 | bytes 6291456 | tf_op jit(solution)/shard_map/dot_general | solution.py:57
  151.5 0.0 copy-done.1
  151.5 0.0 copy-done.4
  151.5 0.0 copy-done.13
  151.5 5.7 %fusion.2 = bf16[1,1024,1024]{2,1,0:T(8,128)(2,1)} fusion(f32[1024,1024]{1,0:T(8,128)S(1)} %copy-done.13, f32[128,8,8,128]{3,2,1,0:T(8,128)S(1)} %bitcast.134, bf16[2,1024,1024]{1,2,0:T(8,128)(2,1)} %collective-permute-done, bf16[128,8,8,128]{3,2,1,0:T(8,128)(2,1)S(1)} %bitcast.138), kind=kOutput, calls=%fused_computation.10 | convolution fusion | flops 2150629376 | bytes 14680064 | tf_op jit(solution)/shard_map/dot_general | solution.py:56
  (513 shorter events, 4.6 us)
Async XLA Ops:
  7.2 7.0 %copy-start = (bf16[1,1024,1024]{2,1,0:T(8,128)(2,1)S(1)}, bf16[1,1024,1024]{2,1,0:T(8,128)(2,1)}, u32[]{:S(2)}) copy-start(bf16[1,1024,1024]{2,1,0:T(8,128)(2,1)} %param.15) | copy-start | bytes 6291460
  7.2 1.7 %copy-start.10 = (s32[2,24]{1,0:T(2,128)S(1)}, s32[2,24]{1,0:T(2,128)}, u32[]{:S(2)}) copy-start(s32[2,24]{1,0:T(2,128)} %param.10) | copy-start | bytes 580
  7.2 122.4 %all-gather.3.cloned.1.call-start = ((), (), s32[]{:S(2)}) async-start(), calls=%async_computation | async-start | bytes 1052672 | tf_op jit(solution)/shard_map/all_gather | solution.py:19
  14.2 5.5 %copy-start.2 = (bf16[8,8,128,128]{3,1,2,0:T(8,128)(2,1)S(1)}, bf16[8,8,128,128]{3,1,2,0:T(8,128)(2,1)}, u32[]{:S(2)}) copy-start(bf16[8,8,128,128]{3,1,2,0:T(8,128)(2,1)} %copy.30) | copy-start | bytes 6291460
  18.3 1.3 copy-start.5
  23.3 2.1 %copy-start.11 = (s32[2,24]{1,0:T(2,128)S(1)}, s32[2,24]{1,0:T(2,128)}, u32[]{:S(2)}) copy-start(s32[2,24]{1,0:T(2,128)} %param.12) | copy-start | bytes 580
  26.8 2.4 %copy-start.6 = (bf16[1024,1024]{1,0:T(8,128)(2,1)S(1)}, bf16[1024,1024]{1,0:T(8,128)(2,1)}, u32[]{:S(2)}) copy-start(bf16[1024,1024]{1,0:T(8,128)(2,1)} %copy-done.5) | copy-start | bytes 6291460
  29.2 2.7 %copy-start.7 = (bf16[1024,1024]{1,0:T(8,128)(2,1)}, bf16[1024,1024]{1,0:T(8,128)(2,1)S(1)}, u32[]{:S(2)}) copy-start(bf16[1024,1024]{1,0:T(8,128)(2,1)S(1)} %fusion.17) | copy-start | bytes 6291460
  31.9 113.5 %collective-permute-start = (bf16[2,1024,1024]{1,2,0:T(8,128)(2,1)}, bf16[2,1024,1024]{1,2,0:T(8,128)(2,1)}, u32[]{:S(2)}, u32[]{:S(2)}) collective-permute-start(bf16[2,1024,1024]{1,2,0:T(8,128)(2,1)} %pad_maximum_fusion), channel_id=1, source_target_pairs={{0,1},{1,2},{2,3},{3,4},{4,5},{5,6},{6,7},{7,8},{8,9},{9,10},{10,1... | collective-permute-start | bytes 12582920 | tf_op jit(solution)/shard_map/ppermute | solution.py:14
  34.9 1.7 %copy-start.9 = (bf16[1,24,128,128]{3,2,1,0:T(8,128)(2,1)S(1)}, bf16[1,24,128,128]{3,2,1,0:T(8,128)(2,1)}, u32[]{:S(2)}) copy-start(bf16[1,24,128,128]{3,2,1,0:T(8,128)(2,1)} %param.13) | copy-start | bytes 2359300
  34.9 1.7 %copy-start.12 = (s32[1,24]{1,0:T(1,128)S(1)}, s32[1,24]{1,0:T(1,128)}, u32[]{:S(2)}) copy-start(s32[1,24]{1,0:T(1,128)} %param.14) | copy-start | bytes 292
  37.5 2.4 %copy-start.3 = (bf16[8,8,128,128]{3,1,2,0:T(8,128)(2,1)S(1)}, bf16[8,8,128,128]{3,1,2,0:T(8,128)(2,1)}, u32[]{:S(2)}) copy-start(bf16[8,8,128,128]{3,1,2,0:T(8,128)(2,1)} %copy.30) | copy-start | bytes 6291460
  37.5 3.7 %copy-start.8 = (bf16[1024,1024]{1,0:T(8,128)(2,1)S(1)}, bf16[1024,1024]{1,0:T(8,128)(2,1)}, u32[]{:S(2)}) copy-start(bf16[1024,1024]{1,0:T(8,128)(2,1)} %copy-done.7) | copy-start | bytes 6291460
  145.4 6.1 %copy-start.1 = (f32[8,128,8,128]{3,2,1,0:T(8,128)S(1)}, f32[8,128,8,128]{3,2,1,0:T(8,128)}, u32[]{:S(2)}) copy-start(f32[8,128,8,128]{3,2,1,0:T(8,128)} %copy.28) | copy-start | bytes 12582916
  145.4 6.1 %copy-start.4 = (bf16[8,8,128,128]{3,1,2,0:T(8,128)(2,1)S(1)}, bf16[8,8,128,128]{3,1,2,0:T(8,128)(2,1)}, u32[]{:S(2)}) copy-start(bf16[8,8,128,128]{3,1,2,0:T(8,128)(2,1)} %copy.34) | copy-start | bytes 6291460
  145.4 6.1 %copy-start.13 = (f32[1024,1024]{1,0:T(8,128)S(1)}, f32[1024,1024]{1,0:T(8,128)}, u32[]{:S(2)}) copy-start(f32[1024,1024]{1,0:T(8,128)} %fusion.13) | copy-start | bytes 12582916
Sparse Core Ops, SparseCore 0:
  24.1 105.4 all-gather.2
where the time goes:
time: 166 us; the launch traced here: 164 us
  waiting for transfers between devices  84 us (51%)
  matrix products  30.8 us (19%)
  local copies, waits for them, and re-layouts  18 us (11%)
  between operations  14.3 us (9%)
  loops' own time  9.26 us (6%)
  other arithmetic  5.55 us (3%)
  starting transfers between devices  2.13 us (1%)
    all_gather x1, waiting for transfers between devices, carried_in(): pieces = lax.all_gather(value, axis)  84 us
    another operation x1, loops' own time, carried_in(): return lax.fori_loop(0, count - 1, turn, so_far)  9.26 us
    dot_general x1, matrix products, local(): jnp.dot(even_down, below[1], preferred_element_type=jnp.float32)  6.06 us
    dot_general x1, matrix products, local(): below_low = jnp.dot(even_down, below[0], preferred_element_type=jnp.float32)  5.68 us
    reshape x4, local copies, waits for them, and re-layouts, expand_tiles(): blocks.reshape(NT, NT, TILE, TILE).transpose(0, 2, 1, 3)  5.5 us
    dot_general x5, matrix products, expand_tiles(): jnp.einsum('pk,kij->pij', onehot, tiles, preferred_element_type=jnp.float32)  4.52 us
    dot_general x1, matrix products, local(): up_high = jnp.dot(even_up, own[1], preferred_element_type=jnp.float32)  4.34 us
    dot_general x1, matrix products, odd_products(): jnp.dot(inverse, expand_tiles(up_block, up_places), preferred_element_typ...  4.12 us
  transfers between devices with their start and end apart: 2, of which 1 were waited for; matrix products, arithmetic and copies ran while one was open for 15% of the time, Pallas kernels for 0%

commit v1 on v0

v1 whole, which is shorter than its diff:
```python
import functools

import jax
import jax.numpy as jnp
from jax import lax
from jax.experimental import pallas as pl
from jax.experimental.pallas import tpu as pltpu
from jax.sharding import PartitionSpec as P

TILE = 128
NT = 8
P_SIZE = 1024
KT = 24
WIDE = 256
AXES = ("grp", "lev")
MESH = pl.DeviceIdType.MESH
F32 = jnp.float32
BF16 = jnp.bfloat16


def vmem():
    return pl.BlockSpec(memory_space=pltpu.VMEM)


def smem():
    return pl.BlockSpec(memory_space=pltpu.SMEM)


def expand(dense, tiles, at, row, tile_row=None):
    dense[...] = jnp.zeros_like(dense)

    def place(k, carry):
        p = at[row, k]
        r = pl.multiple_of((p // NT) * TILE, TILE)
        c = pl.multiple_of((p % NT) * TILE, TILE)
        tile = tiles[k] if tile_row is None else tiles[tile_row, k]
        dense[pl.ds(r, TILE), pl.ds(c, TILE)] = tile
        return carry

    lax.fori_loop(0, KT, place, 0, unroll=4)


def column_blocks(body):
    def step(b, carry):
        body(pl.ds(pl.multiple_of(b * WIDE, WIDE), WIDE))
        return carry

    lax.fori_loop(0, P_SIZE // WIDE, step, 0)


def mm(a, b):
    return jnp.dot(a, b, preferred_element_type=F32)


def own_kernel(
    up_at, down_at, diag_at, up, down, diag, inv, new_up, rest, term, wide, prod, even
):
    level = lax.axis_index("grp") * lax.axis_size("lev") + lax.axis_index("lev")
    count = lax.axis_size("grp") * lax.axis_size("lev")
    weight = (count + 2 * level).astype(F32) / count
    expand(wide, up, up_at, 1, 1)

    def first(cols):
        prod[:, cols] = mm(inv[0], wide[:, cols]).astype(BF16)

    column_blocks(first)
    expand(even, up, up_at, 0, 0)

    def second(cols):
        out = (-mm(even[...], prod[:, cols])).astype(BF16)
        new_up[0, :, cols] = out
        mean = jnp.sum(out.astype(F32), axis=0, keepdims=True) / P_SIZE
        term[:, cols] = weight * mean

    column_blocks(second)
    expand(wide, down, down_at, 1, 1)
    column_blocks(first)
    expand(wide, diag, diag_at, 0, 0)

    def third(cols):
        rest[:, cols] = wide[:, cols].astype(F32) - mm(even[...], prod[:, cols])

    column_blocks(third)


def own_products(up_at, down_at, diag_at, up, down, diag, inv):
    return pl.pallas_call(
        own_kernel,
        name="own_products",
        out_shape=(
            jax.ShapeDtypeStruct((1, P_SIZE, P_SIZE), BF16),
            jax.ShapeDtypeStruct((P_SIZE, P_SIZE), F32),
            jax.ShapeDtypeStruct((1, P_SIZE), F32),
        ),
        in_specs=[smem()] * 3 + [vmem()] * 4,
        out_specs=(vmem(),) * 3,
        scratch_shapes=[pltpu.VMEM((P_SIZE, P_SIZE), BF16)] * 3,
        compiler_params=pltpu.CompilerParams(vmem_limit_bytes=32 << 20),
        cost_estimate=pl.CostEstimate(
            flops=4 * 2 * P_SIZE**3, bytes_accessed=12 << 20, transcendentals=0
        ),
    )(up_at, down_at, diag_at, up, down, diag, inv)


def scan_kernel(bits, term, out, total, incoming, send_sem, recv_sem):
    inner = lax.axis_size("lev")
    me = lax.axis_index("grp") * inner + lax.axis_index("lev")
    partners, upper = [], []
    for d in range(bits):
        bit = (me // 2**d) % 2
        other = me + 2**d * (1 - 2 * bit)
        upper.append(bit)
        partners.append((other // inner, other % inner))
    barrier = pltpu.get_barrier_semaphore()
    for p in partners:
        pl.semaphore_signal(barrier, inc=1, device_id=p, device_id_type=MESH)
    pl.semaphore_wait(barrier, bits)
    out[...] = term[...]
    total[0] = term[...]
    for d in range(bits):
        copy = pltpu.make_async_remote_copy(
            src_ref=total.at[d],
            dst_ref=incoming.at[d],
            send_sem=send_sem.at[d],
            recv_sem=recv_sem.at[d],
            device_id=partners[d],
            device_id_type=MESH,
        )
        copy.start()
        copy.wait()
        got = incoming[d]
        out[...] += got * upper[d].astype(F32)
        if d < bits - 1:
            total[d + 1] = total[d] + got


def scan_terms(term, count):
    bits = count.bit_length() - 1
    return pl.pallas_call(
        functools.partial(scan_kernel, bits),
        name="scan_terms",
        out_shape=jax.ShapeDtypeStruct((1, P_SIZE), F32),
        in_specs=[vmem()],
        out_specs=vmem(),
        scratch_shapes=[
            pltpu.VMEM((bits, 1, P_SIZE), F32),
            pltpu.VMEM((bits, 1, P_SIZE), F32),
            pltpu.SemaphoreType.DMA((bits,)),
            pltpu.SemaphoreType.DMA((bits,)),
        ],
        compiler_params=pltpu.CompilerParams(
            collective_id=0, has_side_effects=True, vmem_limit_bytes=4 << 20
        ),
    )(term)


def left_kernel(at, tiles, inv, out, even):
    expand(even, tiles, at, 0, 0)

    def step(cols):
        out[:, cols] = mm(even[...], inv[0, :, cols]).astype(BF16)

    column_blocks(step)


def left_product(down_at, down, inv):
    return pl.pallas_call(
        left_kernel,
        name="left_product",
        out_shape=jax.ShapeDtypeStruct((P_SIZE, P_SIZE), BF16),
        in_specs=[smem(), vmem(), vmem()],
        out_specs=vmem(),
        scratch_shapes=[pltpu.VMEM((P_SIZE, P_SIZE), BF16)],
        compiler_params=pltpu.CompilerParams(vmem_limit_bytes=16 << 20),
        cost_estimate=pl.CostEstimate(
            flops=2 * P_SIZE**3, bytes_accessed=5 << 20, transcendentals=0
        ),
    )(down_at, down, inv)


def diag_kernel(at, left, tiles, rest, out, wide):
    expand(wide, tiles, at, 0)

    def step(cols):
        out[0, :, cols] = (rest[:, cols] - mm(left[...], wide[:, cols])).astype(BF16)

    column_blocks(step)


def down_kernel(at, left, tiles, out, wide):
    expand(wide, tiles, at, 1)

    def step(cols):
        out[0, :, cols] = (-mm(left[...], wide[:, cols])).astype(BF16)

    column_blocks(step)


def right_product(kernel, name, at, *operands):
    return pl.pallas_call(
        kernel,
        name=name,
        out_shape=jax.ShapeDtypeStruct((1, P_SIZE, P_SIZE), BF16),
        in_specs=[smem()] + [vmem()] * len(operands),
        out_specs=vmem(),
        scratch_shapes=[pltpu.VMEM((P_SIZE, P_SIZE), BF16)],
        compiler_params=pltpu.CompilerParams(vmem_limit_bytes=16 << 20),
        cost_estimate=pl.CostEstimate(
            flops=2 * P_SIZE**3, bytes_accessed=5 << 20, transcendentals=0
        ),
    )(at, *operands)


def local(count, up_tiles, up_at, down_tiles, down_at, diag_tiles, diag_at, odd_inverse):
    route = [(i, i + 1) for i in range(count - 1)]

    def passed(block):
        return lax.ppermute(block, AXES, route)

    inv_below = passed(odd_inverse)
    at_below = passed(jnp.stack([up_at[1], down_at[1]]))
    up_below = passed(up_tiles[1])
    down_below = passed(down_tiles[1])
    new_up, rest, term = own_products(
        up_at, down_at, diag_at, up_tiles, down_tiles, diag_tiles, odd_inverse
    )
    sums = scan_terms(term, count)
    left = left_product(down_at, down_tiles, inv_below)
    new_diag = right_product(diag_kernel, "diag", at_below, left, up_below, rest)
    new_down = right_product(down_kernel, "down", at_below, left, down_below)
    return new_diag, new_up, new_down, sums


def solution(mesh):
    count = mesh.shape["grp"] * mesh.shape["lev"]
    return jax.shard_map(
        functools.partial(local, count),
        mesh=mesh,
        in_specs=(
            P(AXES, None, None, None),
            P(AXES, None),
            P(AXES, None, None, None),
            P(AXES, None),
            P(AXES, None, None, None),
            P(AXES, None),
            P(AXES, None, None),
        ),
        out_specs=(
            P(AXES, None, None),
            P(AXES, None, None),
            P(AXES, None, None),
            P(AXES, None),
        ),
        check_vma=False,
    )
```

time: 166 us -> 82.9 us (0.50)
  the two profiles are of different devices: /device:TPU:8 before, /device:TPU:1 now
where the time goes in v1:
time: 82.9 us; the launch traced here: 82.5 us
  Pallas kernels  61.7 us (74%)
  starting transfers between devices  13 us (16%)
  local copies, waits for them, and re-layouts  7.08 us (9%)
    pallas_call x1, Pallas kernels, scan_terms(): pl.pallas_call(functools.partial(scan_kernel, bits), name='scan_terms', o...  33.3 us
    pallas_call x1, Pallas kernels, own_products(): pl.pallas_call(own_kernel, name='own_products', out_shape=(jax.ShapeDtype...  14.1 us
    ppermute x4, starting transfers between devices, passed(): return lax.ppermute(block, AXES, route)  13 us
    pallas_call x2, Pallas kernels, right_product(): pl.pallas_call(kernel, name=name, out_shape=jax.ShapeDtypeStruct((1, P_SI...  10.4 us
    pallas_call x1, Pallas kernels, left_product(): pl.pallas_call(left_kernel, name='left_product', out_shape=jax.ShapeDtype...  3.83 us
    unnamed x15, local copies, waits for them, and re-layouts  3.34 us
  transfers between devices with their start and end apart: 4, of which 0 were waited for; matrix products, arithmetic and copies ran while one was open for 5% of the time, Pallas kernels for 68%

profile of v1, /device:TPU:1, one launch (start us, length us, event | category | flops | bytes accessed | tf_op | source)
XLA Modules:
  0.0 82.5 jit_solution(18181369029115975164)
XLA Ops:
  0.6 0.0 copy-start.4
  0.6 0.0 copy-start.5
  0.7 0.0 copy-start
  0.7 0.0 copy-start.1
  0.7 0.0 copy-start.6
  0.7 5.2 %collective-permute-start.1 = (bf16[1,1024,1024]{2,1,0:T(8,128)(2,1)}, bf16[1,1024,1024]{2,1,0:T(8,128)(2,1)S(1)}, u32[]{:S(2)}, u32[]{:S(2)}) collective-permute-start(bf16[1,1024,1024]{2,1,0:T(8,128)(2,1)} %inv.1), channel_id=1, source_target_pairs={{0,1},{1,2},{2,3},{3,4},{4,5},{5,6},{6,7},{7,8},{8,9},{9,10},{10,1... | collective-permute-start | bytes 6291464 | tf_op jit(solution)/shard_map/ppermute | solution.py:218
  5.9 0.7 slice.12
  6.6 0.7 slice.13
  7.3 1.9 %collective-permute-start = (s32[2,24]{1,0:T(2,128)S(1)}, s32[2,24]{1,0:T(2,128)S(1)}, u32[]{:S(2)}, u32[]{:S(2)}) collective-permute-start(s32[2,24]{1,0:T(2,128)S(1)} %pad_add_fusion), channel_id=1, source_target_pairs={{0,1},{1,2},{2,3},{3,4},{4,5},{5,6},{6,7},{7,8},{8,9},{9,10},{10,1... | collective-permute-start | bytes 584 | tf_op jit(solution)/shard_map/ppermute | solution.py:218
  9.2 1.2 %slice_bitcast_fusion.1 = bf16[24,128,128]{2,1,0:T(8,128)(2,1)S(1)} fusion(bf16[2,24,128,128]{3,2,1,0:T(8,128)(2,1)} %up.1), kind=kLoop, calls=%fused_computation.1 | loop fusion | bytes 1572864 | tf_op jit(solution)/shard_map/squeeze | solution.py:222
  10.4 3.9 %collective-permute-start.2 = (bf16[24,128,128]{2,1,0:T(8,128)(2,1)S(1)}, bf16[24,128,128]{2,1,0:T(8,128)(2,1)S(1)}, u32[]{:S(2)}, u32[]{:S(2)}) collective-permute-start(bf16[24,128,128]{2,1,0:T(8,128)(2,1)S(1)} %slice_bitcast_fusion.1), channel_id=1, source_target_pairs={{0,1},{1,2},{2,3},{3,4},{4,5},{5,6},{6,7},{7,8},{8,9},{9,10},{10,1... | collective-permute-start | bytes 2359304 | tf_op jit(solution)/shard_map/ppermute | solution.py:218
  14.3 1.2 %slice_bitcast_fusion = bf16[24,128,128]{2,1,0:T(8,128)(2,1)S(1)} fusion(bf16[2,24,128,128]{3,2,1,0:T(8,128)(2,1)} %down.2), kind=kLoop, calls=%fused_computation | loop fusion | bytes 1572864 | tf_op jit(solution)/shard_map/squeeze | solution.py:223
  15.5 1.9 %collective-permute-start.3 = (bf16[24,128,128]{2,1,0:T(8,128)(2,1)S(1)}, bf16[24,128,128]{2,1,0:T(8,128)(2,1)S(1)}, u32[]{:S(2)}, u32[]{:S(2)}) collective-permute-start(bf16[24,128,128]{2,1,0:T(8,128)(2,1)S(1)} %slice_bitcast_fusion), channel_id=1, source_target_pairs={{0,1},{1,2},{2,3},{3,4},{4,5},{5,6},{6,7},{7,8},{8,9},{9,10},{10,1... | collective-permute-start | bytes 2359304 | tf_op jit(solution)/shard_map/ppermute | solution.py:218
  17.4 0.0 copy-done.4
  17.5 0.0 copy-done.5
  17.5 0.0 copy-done
  17.5 0.0 copy-done.1
  17.5 0.0 copy-done.6
  17.5 0.0 copy-start.2
  17.5 1.6 %copy-done.2 = bf16[1,1024,1024]{2,1,0:T(8,128)(2,1)S(1)} copy-done((bf16[1,1024,1024]{2,1,0:T(8,128)(2,1)S(1)}, bf16[1,1024,1024]{2,1,0:T(8,128)(2,1)}, u32[]{:S(2)}) %copy-start.2) | copy-done | bytes 2097176
  19.1 0.0 copy-start.3
  19.1 1.1 %copy-done.3 = bf16[1,24,128,128]{3,2,1,0:T(8,128)(2,1)S(1)} copy-done((bf16[1,24,128,128]{3,2,1,0:T(8,128)(2,1)S(1)}, bf16[1,24,128,128]{3,2,1,0:T(8,128)(2,1)}, u32[]{:S(2)}) %copy-start.3) | copy-done | bytes 786456
  20.2 14.1 %own_products.1 = (bf16[1,1024,1024]{2,1,0:T(8,128)(2,1)}, f32[1024,1024]{1,0:T(8,128)S(1)}, f32[1,1024]{1,0:T(1,128)S(1)}) custom-call(s32[2,24]{1,0:T(2,128)S(1)} %copy-done.4, s32[2,24]{1,0:T(2,128)S(1)} %copy-done.5, s32[1,24]{1,0:T(1,128)S(1)} %copy-done.6, bf16[2,24,128,128]{3,2,1,0:T(8,128)(2,1)S(1)} %copy-done, ...), custom_call_target="tpu_custom_call" | custom-call | flops 8589934592 | bytes 12582912 | tf_op jit(solution)/shard_map/own_products/pallas_call | solution.py:87
  34.3 33.3 %scan_terms.1 = f32[1,1024]{1,0:T(1,128)S(1)} custom-call(f32[1,1024]{1,0:T(1,128)S(1)} %get-tuple-element.9.term), custom_call_target="tpu_custom_call" | custom-call | tf_op jit(solution)/shard_map/scan_terms/pallas_call | solution.py:139
  67.7 0.0 collective-permute-done.1.inv
  67.7 3.8 %left_product.1.left = bf16[1024,1024]{1,0:T(8,128)(2,1)S(1)} custom-call(s32[2,24]{1,0:T(2,128)S(1)} %copy-done.5, bf16[2,24,128,128]{3,2,1,0:T(8,128)(2,1)S(1)} %copy-done.1, bf16[1,1024,1024]{2,1,0:T(8,128)(2,1)S(1)} %collective-permute-done.1.inv), custom_call_target="tpu_custom_call" | custom-call | flops 2147483648 | bytes 5242880 | tf_op jit(solution)/shard_map/left_product/pallas_call | solution.py:167
  71.5 0.0 collective-permute-done.at
  71.5 0.0 collective-permute-done.3.tiles
  71.5 5.2 %down.3 = bf16[1,1024,1024]{2,1,0:T(8,128)(2,1)} custom-call(s32[2,24]{1,0:T(2,128)S(1)} %collective-permute-done.at, bf16[1024,1024]{1,0:T(8,128)(2,1)S(1)} %left_product.1.left, bf16[24,128,128]{2,1,0:T(8,128)(2,1)S(1)} %collective-permute-done.3.tiles), custom_call_target="tpu_custom_call" | custom-call | flops 2147483648 | bytes 5242880 | tf_op jit(solution)/shard_map/down/pallas_call | solution.py:200
  76.8 0.0 collective-permute-done.2.tiles
  76.8 5.2 %diag.3 = bf16[1,1024,1024]{2,1,0:T(8,128)(2,1)} custom-call(s32[2,24]{1,0:T(2,128)S(1)} %collective-permute-done.at, bf16[1024,1024]{1,0:T(8,128)(2,1)S(1)} %left_product.1.left, bf16[24,128,128]{2,1,0:T(8,128)(2,1)S(1)} %collective-permute-done.2.tiles, f32[1024,1024]{1,0:T(8,128)S(1)} %get-tuple-element.7.rest), custom_call_target="tpu_custom_call" | custom-call | flops 2147483648 | bytes 5242880 | tf_op jit(solution)/shard_map/diag/pallas_call | solution.py:200
  81.9 0.6 copy.12
  (1 shorter events, 0.0 us)
Async XLA Ops:
  0.6 16.8 %copy-start.4 = (s32[2,24]{1,0:T(2,128)S(1)}, s32[2,24]{1,0:T(2,128)}, u32[]{:S(2)}) copy-start(s32[2,24]{1,0:T(2,128)} %up_at.1) | copy-start | bytes 580
  0.6 16.8 %copy-start.5 = (s32[2,24]{1,0:T(2,128)S(1)}, s32[2,24]{1,0:T(2,128)}, u32[]{:S(2)}) copy-start(s32[2,24]{1,0:T(2,128)} %down_at.1) | copy-start | bytes 580
  0.7 16.8 %copy-start = (bf16[2,24,128,128]{3,2,1,0:T(8,128)(2,1)S(1)}, bf16[2,24,128,128]{3,2,1,0:T(8,128)(2,1)}, u32[]{:S(2)}) copy-start(bf16[2,24,128,128]{3,2,1,0:T(8,128)(2,1)} %up.1) | copy-start | bytes 4718596
  0.7 16.8 %copy-start.1 = (bf16[2,24,128,128]{3,2,1,0:T(8,128)(2,1)S(1)}, bf16[2,24,128,128]{3,2,1,0:T(8,128)(2,1)}, u32[]{:S(2)}) copy-start(bf16[2,24,128,128]{3,2,1,0:T(8,128)(2,1)} %down.2) | copy-start | bytes 4718596
  0.7 16.8 %copy-start.6 = (s32[1,24]{1,0:T(1,128)S(1)}, s32[1,24]{1,0:T(1,128)}, u32[]{:S(2)}) copy-start(s32[1,24]{1,0:T(1,128)} %diag_at.1) | copy-start | bytes 292
  0.7 67.0 %collective-permute-start.1 = (bf16[1,1024,1024]{2,1,0:T(8,128)(2,1)}, bf16[1,1024,1024]{2,1,0:T(8,128)(2,1)S(1)}, u32[]{:S(2)}, u32[]{:S(2)}) collective-permute-start(bf16[1,1024,1024]{2,1,0:T(8,128)(2,1)} %inv.1), channel_id=1, source_target_pairs={{0,1},{1,2},{2,3},{3,4},{4,5},{5,6},{6,7},{7,8},{8,9},{9,10},{10,1... | collective-permute-start | bytes 6291464 | tf_op jit(solution)/shard_map/ppermute | solution.py:218
  7.3 64.3 %collective-permute-start = (s32[2,24]{1,0:T(2,128)S(1)}, s32[2,24]{1,0:T(2,128)S(1)}, u32[]{:S(2)}, u32[]{:S(2)}) collective-permute-start(s32[2,24]{1,0:T(2,128)S(1)} %pad_add_fusion), channel_id=1, source_target_pairs={{0,1},{1,2},{2,3},{3,4},{4,5},{5,6},{6,7},{7,8},{8,9},{9,10},{10,1... | collective-permute-start | bytes 584 | tf_op jit(solution)/shard_map/ppermute | solution.py:218
  10.4 66.4 %collective-permute-start.2 = (bf16[24,128,128]{2,1,0:T(8,128)(2,1)S(1)}, bf16[24,128,128]{2,1,0:T(8,128)(2,1)S(1)}, u32[]{:S(2)}, u32[]{:S(2)}) collective-permute-start(bf16[24,128,128]{2,1,0:T(8,128)(2,1)S(1)} %slice_bitcast_fusion.1), channel_id=1, source_target_pairs={{0,1},{1,2},{2,3},{3,4},{4,5},{5,6},{6,7},{7,8},{8,9},{9,10},{10,1... | collective-permute-start | bytes 2359304 | tf_op jit(solution)/shard_map/ppermute | solution.py:218
  15.5 56.0 %collective-permute-start.3 = (bf16[24,128,128]{2,1,0:T(8,128)(2,1)S(1)}, bf16[24,128,128]{2,1,0:T(8,128)(2,1)S(1)}, u32[]{:S(2)}, u32[]{:S(2)}) collective-permute-start(bf16[24,128,128]{2,1,0:T(8,128)(2,1)S(1)} %slice_bitcast_fusion), channel_id=1, source_target_pairs={{0,1},{1,2},{2,3},{3,4},{4,5},{5,6},{6,7},{7,8},{8,9},{9,10},{10,1... | collective-permute-start | bytes 2359304 | tf_op jit(solution)/shard_map/ppermute | solution.py:218
  17.5 1.6 %copy-start.2 = (bf16[1,1024,1024]{2,1,0:T(8,128)(2,1)S(1)}, bf16[1,1024,1024]{2,1,0:T(8,128)(2,1)}, u32[]{:S(2)}) copy-start(bf16[1,1024,1024]{2,1,0:T(8,128)(2,1)} %inv.1) | copy-start | bytes 6291460
  19.1 1.1 %copy-start.3 = (bf16[1,24,128,128]{3,2,1,0:T(8,128)(2,1)S(1)}, bf16[1,24,128,128]{3,2,1,0:T(8,128)(2,1)}, u32[]{:S(2)}) copy-start(bf16[1,24,128,128]{3,2,1,0:T(8,128)(2,1)} %diag.2) | copy-start | bytes 2359300

commit v2 on v0

v2 whole, which is shorter than its diff:
```python
import functools

import jax
import jax.numpy as jnp
from jax import lax
from jax.experimental import pallas as pl
from jax.experimental.pallas import tpu as pltpu
from jax.sharding import PartitionSpec as P

TILE = 128
NT = 8
P_SIZE = 1024
KT = 24
HALF = KT // 2
WIDE = 256
RADIX = 4
AXES = ("grp", "lev")
MESH = pl.DeviceIdType.MESH
F32 = jnp.float32
BF16 = jnp.bfloat16
I32 = jnp.int32
INV, UP, PLACE, DOWN_A, DOWN_B, HOP_1, HOP_2, HOP_3, SCAN = range(9)


def mm(a, b):
    return jnp.dot(a, b, preferred_element_type=F32)


def column_blocks(body):
    def step(b, carry):
        body(pl.ds(pl.multiple_of(b * WIDE, WIDE), WIDE))
        return carry

    lax.fori_loop(0, P_SIZE // WIDE, step, 0)


def expand(dense, tile_of, slots, row):
    def tile_row(r, carry):
        rows = pl.ds(pl.multiple_of(r * TILE, TILE), TILE)
        for c in range(NT):
            slot = slots[row, r * NT + c]
            tile = tile_of(jnp.clip(slot, 0, KT - 1))
            dense[rows, c * TILE : (c + 1) * TILE] = jnp.where(slot >= 0, tile, jnp.zeros_like(tile))
        return carry

    lax.fori_loop(0, NT, tile_row, 0)


def slot_row(places):
    number = lax.broadcasted_iota(I32, (KT, KT), 0)
    lane = lax.broadcasted_iota(I32, (KT, KT), 1)
    spread = jnp.broadcast_to(places, (KT, KT))
    column = jnp.sum(jnp.where(number == lane, spread, 0), axis=1, keepdims=True)
    position = lax.broadcasted_iota(I32, (KT, TILE), 1)
    index = lax.broadcasted_iota(I32, (KT, TILE), 0) + 1
    hit = jnp.broadcast_to(column, (KT, TILE)) == position
    return jnp.max(jnp.where(hit, index, 0), axis=0, keepdims=True) - 1


def exchange_kernel(
    sizes,
    up_at,
    down_at,
    diag_at,
    up,
    down,
    diag,
    inv,
    left,
    down_in,
    places_in,
    new_up,
    new_diag,
    sums,
    up_at_v,
    down_at_v,
    diag_at_v,
    up_v,
    down_v,
    diag_v,
    inv_v,
    places,
    slots,
    slots_in,
    inv_in,
    up_in,
    hop_1,
    hop_2,
    wide,
    even,
    prod,
    rest,
    total,
    incoming,
    local_sem,
    send_sem,
    recv_sem,
):
    groups, inner, length = sizes
    count = groups * inner
    lev = lax.axis_index("lev")
    grp = lax.axis_index("grp")
    me = grp * inner + lev
    core = lev % 2

    def at(index):
        index = (index + count) % count
        return (index // inner, index % inner)

    def along(distance):
        z = (lev // 2) % length
        return (grp, lev - 2 * z + 2 * ((z + distance + length) % length))

    following, before = at(me + 1), at(me - 1)
    behind, ahead = along(-3), along(3)
    origin_g, origin_l = along(-2)
    target = at(origin_g * inner + origin_l + 1)
    prev_g, prev_l = before
    prev_z = (prev_l // 2) % length
    holder = (prev_g, prev_l - 2 * prev_z + 2 * ((prev_z + 2) % length))
    third_g = core * target[0] + (1 - core) * holder[0]
    third_l = core * target[1] + (1 - core) * holder[1]

    peers = [following, before, behind, ahead, (third_g, third_l)]
    rounds = []
    stride = 1
    while stride < count:
        digit = (me // stride) % RADIX
        others = [
            at(me - digit * stride + ((digit + j) % RADIX) * stride) for j in range(1, RADIX)
        ]
        rounds.append((digit, others))
        peers += others
        stride *= RADIX

    def load(source, target, sem):
        copy = pltpu.make_async_copy(source, target, local_sem.at[sem])
        copy.start()
        return copy

    load_up_at = load(up_at, up_at_v, 0)
    load_down_at = load(down_at, down_at_v, 1)
    load_diag_at = load(diag_at, diag_at_v, 2)
    load_up = load(up, up_v, 3)
    load_inv = load(inv.at[0], inv_v, 4)
    load_down = load(down, down_v, 5)
    load_diag = load(diag.at[0], diag_v, 6)

    barrier = pltpu.get_barrier_semaphore()
    for p in peers:
        pl.semaphore_signal(barrier, inc=1, device_id=p, device_id_type=MESH)
    pl.semaphore_wait(barrier, len(peers))

    def remote(source, target, send, recv, device):
        return pltpu.make_async_remote_copy(
            src_ref=source,
            dst_ref=target,
            send_sem=send_sem.at[send],
            recv_sem=recv_sem.at[recv],
            device_id=device,
            device_id_type=MESH,
        )

    first_half, second_half = pl.ds(0, HALF), pl.ds(HALF, HALF)
    send_hop_1 = remote(down.at[1, second_half], hop_1, HOP_1, HOP_1, behind)
    send_hop_2 = remote(hop_1, hop_2, HOP_2, HOP_2, behind)
    send_hop_3 = remote(hop_2, down_in.at[second_half], HOP_3, DOWN_B, target)
    send_down_b = remote(
        down.at[1, second_half], down_in.at[second_half], DOWN_B, DOWN_B, following
    )
    send_inv = remote(inv.at[0], inv_in, INV, INV, following)
    send_up = remote(up.at[1], up_in, UP, UP, following)
    send_places = remote(places, places_in, PLACE, PLACE, following)
    send_down_a = remote(
        down.at[1, first_half], down_in.at[first_half], DOWN_A, DOWN_A, following
    )

    @pl.when(core == 1)
    def _():
        send_hop_1.start()

    send_inv.start()
    send_up.start()
    load_up_at.wait()
    load_down_at.wait()
    load_diag_at.wait()
    places[...] = jnp.full_like(places, -1)
    places[0:1] = slot_row(up_at_v[1:2])
    places[1:2] = slot_row(down_at_v[1:2])
    places[2:3] = slot_row(up_at_v[0:1])
    places[3:4] = slot_row(down_at_v[0:1])
    places[4:5] = slot_row(diag_at_v[...])
    send_places.start()
    send_down_a.start()

    @pl.when(core == 0)
    def _():
        send_down_b.start()

    load_slots = load(places, slots, 7)
    load_slots.wait()
    load_up.wait()
    expand(wide, lambda s: up_v[1, s], slots, 0)
    load_inv.wait()

    def odd_product(cols):
        prod[:, cols] = mm(inv_v[...], wide[:, cols]).astype(BF16)

    column_blocks(odd_product)
    expand(even, lambda s: up_v[0, s], slots, 2)
    weight = (count + 2 * me).astype(F32) / count

    def up_product(cols):
        out = (-mm(even[...], prod[:, cols])).astype(BF16)
        new_up[:, cols] = out
        mean = jnp.sum(out.astype(F32), axis=0, keepdims=True) / P_SIZE
        total[0, :, cols] = weight * mean

    column_blocks(up_product)

    def scan_copies(n):
        return [
            remote(
                total.at[n],
                incoming.at[3 * n + j],
                SCAN + 3 * n + j,
                SCAN + 3 * n + j,
                rounds[n][1][j],
            )
            for j in range(RADIX - 1)
        ]

    def scan_start(n):
        for copy in scan_copies(n):
            copy.start()

    def scan_finish(n):
        for copy in scan_copies(n):
            copy.wait()
        digit = rounds[n][0]
        so_far = total[n]
        for j in range(RADIX - 1):
            got = incoming[3 * n + j]
            so_far = so_far + got
            sums[...] += jnp.where(digit > j, got, jnp.zeros_like(got))
        if n < len(rounds) - 1:
            total[n + 1] = so_far

    sums[...] = total[0]
    scan_start(0)
    load_down.wait()
    expand(wide, lambda s: down_v[1, s], slots, 1)
    column_blocks(odd_product)
    scan_finish(0)
    scan_start(1)
    load_diag.wait()
    expand(wide, lambda s: diag_v[s], slots, 4)

    def rest_product(cols):
        rest[:, cols] = wide[:, cols].astype(F32) - mm(even[...], prod[:, cols])

    column_blocks(rest_product)
    scan_finish(1)
    scan_start(2)
    expand(even, lambda s: down_v[0, s], slots, 3)

    @pl.when(core == 1)
    def _():
        send_hop_1.wait()
        send_hop_2.start()

    scan_finish(2)
    scan_start(3)
    send_inv.wait()

    def left_product(cols):
        out = mm(even[...], inv_in[:, cols])
        left[:, cols] = jnp.where(me > 0, out, jnp.zeros_like(out)).astype(BF16)

    column_blocks(left_product)

    @pl.when(core == 1)
    def _():
        send_hop_2.wait()
        send_hop_3.start()

    scan_finish(3)
    send_places.wait()
    load_slots_in = load(places_in, slots_in, 8)
    load_slots_in.wait()
    send_up.wait()
    expand(wide, lambda s: up_in[s], slots_in, 0)

    def diag_product(cols):
        new_diag[:, cols] = (rest[:, cols] - mm(left[...], wide[:, cols])).astype(BF16)

    column_blocks(diag_product)
    send_down_a.wait()

    @pl.when(core == 1)
    def _():
        send_hop_3.wait_send()

    @pl.when(core == 0)
    def _():
        send_down_b.wait_send()

    send_down_b.wait_recv()


def exchange(sizes, *operands):
    dense = pltpu.VMEM((P_SIZE, P_SIZE), BF16)
    rounds = (sizes[0] * sizes[1]).bit_length() // 2
    vmem = pl.BlockSpec(memory_space=pltpu.VMEM)
    square = jax.ShapeDtypeStruct((P_SIZE, P_SIZE), BF16)
    return pl.pallas_call(
        functools.partial(exchange_kernel, sizes),
        name="exchange",
        out_shape=(
            square,
            jax.ShapeDtypeStruct((KT, TILE, TILE), BF16),
            jax.ShapeDtypeStruct((NT, TILE), I32),
            square,
            square,
            jax.ShapeDtypeStruct((1, P_SIZE), F32),
        ),
        in_specs=[pl.BlockSpec(memory_space=pltpu.HBM)] * 7,
        out_specs=(vmem,) * 6,
        scratch_shapes=[
            pltpu.VMEM((2, KT), I32),
            pltpu.VMEM((2, KT), I32),
            pltpu.VMEM((1, KT), I32),
            pltpu.VMEM((2, KT, TILE, TILE), BF16),
            pltpu.VMEM((2, KT, TILE, TILE), BF16),
            pltpu.VMEM((KT, TILE, TILE), BF16),
            dense,
            pltpu.VMEM((NT, TILE), I32),
            pltpu.SMEM((NT, TILE), I32),
            pltpu.SMEM((NT, TILE), I32),
            dense,
            pltpu.VMEM((KT, TILE, TILE), BF16),
            pltpu.VMEM((HALF, TILE, TILE), BF16),
            pltpu.VMEM((HALF, TILE, TILE), BF16),
            dense,
            dense,
            dense,
            pltpu.VMEM((P_SIZE, P_SIZE), F32),
            pltpu.VMEM((rounds, 1, P_SIZE), F32),
            pltpu.VMEM((3 * rounds, 1, P_SIZE), F32),
            pltpu.SemaphoreType.DMA((9,)),
            pltpu.SemaphoreType.DMA((SCAN + 3 * rounds,)),
            pltpu.SemaphoreType.DMA((SCAN + 3 * rounds,)),
        ],
        compiler_params=pltpu.CompilerParams(
            collective_id=0, has_side_effects=True, vmem_limit_bytes=54 << 20
        ),
    )(*operands)


def finish_kernel(
    places, left, tiles, up_in, diag_in, sums_in, new_diag, new_up, new_down, sums, wide, out, sem
):
    copies = [
        pltpu.make_async_copy(up_in, new_up.at[0], sem.at[0]),
        pltpu.make_async_copy(diag_in, new_diag.at[0], sem.at[1]),
    ]
    for copy in copies:
        copy.start()
    sums[...] = sums_in[...]
    expand(wide, lambda s: tiles[s], places, 1)
    for b in range(P_SIZE // WIDE):
        cols = pl.ds(b * WIDE, WIDE)
        out[:, cols] = (-mm(left[...], wide[:, cols])).astype(BF16)
        copy = pltpu.make_async_copy(out.at[:, cols], new_down.at[0, :, cols], sem.at[2 + b])
        copy.start()
        copies.append(copy)
    for copy in copies:
        copy.wait()


def finish(places, *operands):
    vmem = pl.BlockSpec(memory_space=pltpu.VMEM)
    hbm = pl.BlockSpec(memory_space=pltpu.HBM)
    square = jax.ShapeDtypeStruct((1, P_SIZE, P_SIZE), BF16)
    return pl.pallas_call(
        finish_kernel,
        name="finish",
        out_shape=(square, square, square, jax.ShapeDtypeStruct((1, P_SIZE), F32)),
        in_specs=[pl.BlockSpec(memory_space=pltpu.SMEM)] + [vmem] * 5,
        out_specs=(hbm, hbm, hbm, vmem),
        scratch_shapes=[
            pltpu.VMEM((P_SIZE, P_SIZE), BF16),
            pltpu.VMEM((P_SIZE, P_SIZE), BF16),
            pltpu.SemaphoreType.DMA((2 + P_SIZE // WIDE,)),
        ],
        compiler_params=pltpu.CompilerParams(vmem_limit_bytes=16 << 20),
    )(places, *operands)


def local(sizes, up_tiles, up_at, down_tiles, down_at, diag_tiles, diag_at, odd_inverse):
    left, down_in, places_in, new_up, new_diag, sums = exchange(
        sizes, up_at, down_at, diag_at, up_tiles, down_tiles, diag_tiles, odd_inverse
    )
    return finish(places_in, left, down_in, new_up, new_diag, sums)


def solution(mesh):
    sizes = (mesh.shape["grp"], mesh.shape["lev"], 8)
    return jax.shard_map(
        functools.partial(local, sizes),
        mesh=mesh,
        in_specs=(
            P(AXES, None, None, None),
            P(AXES, None),
            P(AXES, None, None, None),
            P(AXES, None),
            P(AXES, None, None, None),
            P(AXES, None),
            P(AXES, None, None),
        ),
        out_specs=(
            P(AXES, None, None),
            P(AXES, None, None),
            P(AXES, None, None),
            P(AXES, None),
        ),
        check_vma=False,
    )
```

time: 166 us -> 88.8 us (0.53)
  waiting for transfers between devices: 84 us -> 0 us
  Pallas kernels: 0 us -> 80.1 us
  matrix products: 30.8 us -> 0 us
  between operations: 14.3 us -> 0.65 us
  local copies, waits for them, and re-layouts: 18 us -> 7.25 us
  loops' own time: 9.26 us -> 0 us
  other arithmetic: 5.55 us -> 0 us
  starting transfers between devices: 2.13 us -> 0 us
    all_gather x1 -> x0, waiting for transfers between devices: 84 us -> none  [carried_in(): pieces = lax.all_gather(value, axis)]
    pallas_call x0 -> x2, Pallas kernels: none -> 80.1 us  [the longest x1 74.8 us: exchange(): pl.pallas_call(functools.partial(exchange_kernel, sizes), name='exchange'...]
    dot_general x11 -> x0, matrix products: 30.8 us -> none  [the longest x1 6.06 us: local(): jnp.dot(even_down, below[1], preferred_element_type=jnp.float32)]
    another operation x1 -> x0, loops' own time: 9.26 us -> none  [carried_in(): return lax.fori_loop(0, count - 1, turn, so_far)]
    reshape x4 -> x0, local copies, waits for them, and re-layouts: 5.5 us -> none  [expand_tiles(): blocks.reshape(NT, NT, TILE, TILE).transpose(0, 2, 1, 3)]
    unnamed x28 -> x12, local copies, waits for them, and re-layouts: 2.77 us -> 7.25 us
    slice x2 -> x0, local copies, waits for them, and re-layouts: 3.14 us -> none  [the longest x1 1.64 us: local(): up_tiles[1]]
    dynamic_slice x255 -> x0, local copies, waits for them, and re-layouts: 2.82 us -> none  [turn(): longer = join(so_far, pieces[position])]
  transfers between devices with their start and end apart: 2 -> 0, of which waited for: 1 -> 0; matrix products, arithmetic and copies ran while one was open for 15% -> 0% of each run, Pallas kernels for 0% -> 0%
where the time goes in v2:
time: 88.8 us; the launch traced here: 88.1 us
  Pallas kernels  80.1 us (90%)
  local copies, waits for them, and re-layouts  7.25 us (8%)
    pallas_call x1, Pallas kernels, exchange(): pl.pallas_call(functools.partial(exchange_kernel, sizes), name='exchange'...  74.8 us
    unnamed x12, local copies, waits for them, and re-layouts  7.25 us
    pallas_call x1, Pallas kernels, finish(): pl.pallas_call(finish_kernel, name='finish', out_shape=(square, square, s...  5.32 us

profile of v2, /device:TPU:8, one launch (start us, length us, event | category | flops | bytes accessed | tf_op | source)
XLA Modules:
  0.0 88.1 jit_solution(14628159620476309559)
XLA Ops:
  0.6 74.8 %exchange.1 = (bf16[1024,1024]{1,0:T(8,128)(2,1)}, bf16[24,128,128]{2,1,0:T(8,128)(2,1)}, s32[8,128]{1,0:T(8,128)}, bf16[1024,1024]{1,0:T(8,128)(2,1)}, bf16[1024,1024]{1,0:T(8,128)(2,1)}, /*index=5*/f32[1,1024]{1,0:T(1,128)}) custom-call(s32[2,24]{1,0:T(2,128)} %up_at.1, s32[2,24]{1,0:T(2,128)} %down_at.1, s32[1,24]{1,0:T(1,128)} %diag_at.1, ...), custom_call_target="tpu_custom_call" | custom-call | tf_op jit(solution)/shard_map/exchange/pallas_call | solution.py:316
  75.5 0.0 copy-start
  75.5 1.6 %copy-done = bf16[1024,1024]{1,0:T(8,128)(2,1)S(1)} copy-done((bf16[1024,1024]{1,0:T(8,128)(2,1)S(1)}, bf16[1024,1024]{1,0:T(8,128)(2,1)}, u32[]{:S(2)}) %copy-start) | copy-done | bytes 2097176
  77.1 0.0 copy-start.1
  77.1 1.6 %copy-done.1 = bf16[1024,1024]{1,0:T(8,128)(2,1)S(1)} copy-done((bf16[1024,1024]{1,0:T(8,128)(2,1)S(1)}, bf16[1024,1024]{1,0:T(8,128)(2,1)}, u32[]{:S(2)}) %copy-start.1) | copy-done | bytes 2097176
  78.7 0.0 copy-start.2
  78.7 1.6 %copy-done.2 = bf16[1024,1024]{1,0:T(8,128)(2,1)S(1)} copy-done((bf16[1024,1024]{1,0:T(8,128)(2,1)S(1)}, bf16[1024,1024]{1,0:T(8,128)(2,1)}, u32[]{:S(2)}) %copy-start.2) | copy-done | bytes 2097176
  80.2 0.0 copy-start.3
  80.2 1.1 %copy-done.3 = bf16[24,128,128]{2,1,0:T(8,128)(2,1)S(1)} copy-done((bf16[24,128,128]{2,1,0:T(8,128)(2,1)S(1)}, bf16[24,128,128]{2,1,0:T(8,128)(2,1)}, u32[]{:S(2)}) %copy-start.3) | copy-done | bytes 786456
  81.4 0.0 copy-start.4
  81.4 0.7 copy-done.4
  82.1 0.0 copy-start.5
  82.1 0.7 copy-done.5
  82.7 5.3 %finish.1 = (bf16[1,1024,1024]{2,1,0:T(8,128)(2,1)}, bf16[1,1024,1024]{2,1,0:T(8,128)(2,1)}, bf16[1,1024,1024]{2,1,0:T(8,128)(2,1)}, f32[1,1024]{1,0:T(1,128)}) custom-call(s32[8,128]{1,0:T(8,128)S(1)} %copy-done.4, bf16[1024,1024]{1,0:T(8,128)(2,1)S(1)} %copy-done, bf16[24,128,128]{2,1,0:T(8,128)(2,1)S(1)} %copy-done.3, bf16[1024,1024]{1,0:T(8,128)(2,1)S(1)} %copy-done.1, ...), custom_call_target="tpu_custom_call" | custom-call | tf_op jit(solution)/shard_map/finish/pallas_call | solution.py:385
Async XLA Ops:
  75.5 1.6 %copy-start = (bf16[1024,1024]{1,0:T(8,128)(2,1)S(1)}, bf16[1024,1024]{1,0:T(8,128)(2,1)}, u32[]{:S(2)}) copy-start(bf16[1024,1024]{1,0:T(8,128)(2,1)} %get-tuple-element.11.left) | copy-start | bytes 6291460
  77.1 1.6 %copy-start.1 = (bf16[1024,1024]{1,0:T(8,128)(2,1)S(1)}, bf16[1024,1024]{1,0:T(8,128)(2,1)}, u32[]{:S(2)}) copy-start(bf16[1024,1024]{1,0:T(8,128)(2,1)} %get-tuple-element.13.up_in) | copy-start | bytes 6291460
  78.7 1.6 %copy-start.2 = (bf16[1024,1024]{1,0:T(8,128)(2,1)S(1)}, bf16[1024,1024]{1,0:T(8,128)(2,1)}, u32[]{:S(2)}) copy-start(bf16[1024,1024]{1,0:T(8,128)(2,1)} %get-tuple-element.14.diag_in) | copy-start | bytes 6291460
  80.2 1.1 %copy-start.3 = (bf16[24,128,128]{2,1,0:T(8,128)(2,1)S(1)}, bf16[24,128,128]{2,1,0:T(8,128)(2,1)}, u32[]{:S(2)}) copy-start(bf16[24,128,128]{2,1,0:T(8,128)(2,1)} %get-tuple-element.12.tiles) | copy-start | bytes 2359300
  81.4 0.7 copy-start.4
  82.1 0.7 copy-start.5

commit v3 on v2

v3 whole, which is shorter than its diff:
```python
import functools

import jax
import jax.numpy as jnp
from jax import lax
from jax.experimental import pallas as pl
from jax.experimental.pallas import tpu as pltpu
from jax.sharding import PartitionSpec as P

TILE = 128
NT = 8
P_SIZE = 1024
KT = 24
HALF = KT // 2
WIDE = 256
DEPTH = 8
SIDE = 4
STEPS = (1, 2, 4)
AXES = ("grp", "lev")
MESH = pl.DeviceIdType.MESH
F32 = jnp.float32
BF16 = jnp.bfloat16
I32 = jnp.int32
INV, UP, PLACE, DOWN, HOP, PAIR, LINE, COLUMN = 0, 1, 2, 3, 5, 7, 8, 14


def mm(a, b):
    return jnp.dot(a, b, preferred_element_type=F32)


def column_blocks(body):
    def step(b, carry):
        body(pl.ds(pl.multiple_of(b * WIDE, WIDE), WIDE))
        return carry

    lax.fori_loop(0, P_SIZE // WIDE, step, 0)


def expand(dense, tile_of, slots, row, below=KT):
    def tile_row(r, carry):
        rows = pl.ds(pl.multiple_of(r * TILE, TILE), TILE)
        for c in range(NT):
            slot = slots[row, r * NT + c]
            tile = tile_of(jnp.clip(slot, 0, below - 1))
            here = (slot >= 0) & (slot < below)
            dense[rows, c * TILE : (c + 1) * TILE] = jnp.where(here, tile, jnp.zeros_like(tile))
        return carry

    lax.fori_loop(0, NT, tile_row, 0)


def slot_row(places):
    number = lax.broadcasted_iota(I32, (KT, KT), 0)
    lane = lax.broadcasted_iota(I32, (KT, KT), 1)
    spread = jnp.broadcast_to(places, (KT, KT))
    column = jnp.sum(jnp.where(number == lane, spread, 0), axis=1, keepdims=True)
    position = lax.broadcasted_iota(I32, (KT, TILE), 1)
    index = lax.broadcasted_iota(I32, (KT, TILE), 0) + 1
    hit = jnp.broadcast_to(column, (KT, TILE)) == position
    return jnp.max(jnp.where(hit, index, 0), axis=0, keepdims=True) - 1


def exchange_kernel(
    sizes,
    up_at,
    down_at,
    diag_at,
    up,
    down,
    diag,
    inv,
    left,
    down_wide,
    down_in,
    places_in,
    new_up,
    new_diag,
    sums,
    up_at_v,
    down_at_v,
    diag_at_v,
    up_v,
    down_v,
    diag_v,
    inv_v,
    places,
    slots,
    slots_in,
    inv_in,
    up_in,
    first_in,
    hop,
    wide,
    even,
    prod,
    rest,
    term,
    pair,
    pair_in,
    columns_in,
    rising,
    falling,
    rising_in,
    falling_in,
    local_sem,
    send_sem,
    recv_sem,
    near_sem,
    far_sem,
):
    groups, inner = sizes
    count = groups * inner
    lev = lax.axis_index("lev")
    grp = lax.axis_index("grp")
    me = grp * inner + lev
    core = lev % 2
    z = (lev // 2) % DEPTH
    column = me // (2 * DEPTH)
    columns = count // (2 * DEPTH)

    def place_of(index):
        return (index // inner, index % inner)

    def up_line(distance):
        return place_of(me + 2 * distance)

    other_core = place_of(me + 1 - 2 * core)
    same_z = [
        place_of(((column + j) % columns) * 2 * DEPTH + 2 * z + core) for j in range(1, columns)
    ]
    has_next, has_prev = me < count - 1, me > 0
    inside = column < columns - 1
    far_end = (core == 1) & (z == 7) & inside
    second = (core == 1) & (z == 4) & inside
    third = (core == 1) & (z == 1) & inside
    hop_from = (core == 0) & (z == 0) & has_prev
    target = place_of((column + 1) * 2 * DEPTH)
    holder = place_of((column - 1) * 2 * DEPTH + 3)

    def load(source, target, sem):
        copy = pltpu.make_async_copy(source, target, local_sem.at[sem])
        copy.start()
        return copy

    barrier = pltpu.get_barrier_semaphore()

    def tell(device):
        pl.semaphore_signal(barrier, inc=1, device_id=device, device_id_type=MESH)

    def tell_if(condition, device):
        @pl.when(condition)
        def _():
            tell(device)

    tell_if(has_prev, place_of(me - 1))
    tell(other_core)
    tell_if(z >= 1, up_line(-1))
    for step in STEPS:
        tell_if(z + step < DEPTH, up_line(step))
    tell_if(second | third, up_line(3))
    tell_if(hop_from, holder)
    for device in same_z:
        tell(device)

    load_up_at = load(up_at, up_at_v, 0)
    load_down_at = load(down_at, down_at_v, 1)
    load_diag_at = load(diag_at, diag_at_v, 2)
    load_up = load(up, up_v, 3)
    load_inv = load(inv.at[0], inv_v, 4)
    load_down = load(down, down_v, 5)
    load_diag = load(diag.at[0], diag_v, 6)

    expected = len(same_z) + 1
    for condition in (has_next, z < DEPTH - 1, z >= 1, z >= 2, z >= 4, far_end, second, third):
        expected += condition.astype(I32)
    pl.semaphore_wait(barrier, expected)

    def remote(source, target, send, recv, device):
        return pltpu.make_async_remote_copy(
            src_ref=source,
            dst_ref=target,
            send_sem=send_sem.at[send],
            recv_sem=recv_sem.at[recv],
            device_id=device,
            device_id_type=MESH,
        )

    halves = [pl.ds(c * HALF, HALF) for c in range(2)]
    following = place_of(me + 1)
    send_inv = remote(inv.at[0], inv_in, INV, INV, following)
    send_up = remote(up.at[1], up_in, UP, UP, following)
    send_places = remote(places, places_in, PLACE, PLACE, following)
    send_down = [
        remote(down.at[1, h], landing, DOWN + c, DOWN + c, following)
        for c, (h, landing) in enumerate(zip(halves, (first_in, down_in)))
    ]
    send_back = [
        remote(down.at[1, h], hop.at[h], HOP + c, HOP + c, up_line(-3))
        for c, h in enumerate(halves)
    ]
    send_on = [
        remote(hop.at[h], hop.at[h], HOP + c, HOP + c, up_line(-3)) for c, h in enumerate(halves)
    ]
    send_home = [
        remote(hop.at[h], landing, HOP + c, DOWN + c, target)
        for c, (h, landing) in enumerate(zip(halves, (first_in, down_in)))
    ]

    @pl.when(far_end)
    def _():
        for copy in send_back:
            copy.start()

    @pl.when(has_next)
    def _():
        send_inv.start()
        send_up.start()

    load_up_at.wait()
    load_down_at.wait()
    load_diag_at.wait()
    places[...] = jnp.full_like(places, -1)
    places[0:1] = slot_row(up_at_v[1:2])
    places[1:2] = slot_row(down_at_v[1:2])
    places[2:3] = slot_row(up_at_v[0:1])
    places[3:4] = slot_row(down_at_v[0:1])
    places[4:5] = slot_row(diag_at_v[...])
    places[5:6, 0:KT] = down_at_v[1:2]

    @pl.when(has_next)
    def _():
        send_places.start()

    @pl.when(has_next & ~far_end)
    def _():
        for copy in send_down:
            copy.start()

    @pl.when(z >= 1)
    def _():
        pl.semaphore_signal(near_sem, inc=1, device_id=up_line(-1), device_id_type=MESH)

    @pl.when(me == 0)
    def _():
        inv_in[...] = jnp.zeros_like(inv_in)
        up_in[...] = jnp.zeros_like(up_in)
        first_in[...] = jnp.zeros_like(first_in)
        down_in[...] = jnp.zeros_like(down_in)
        places_in[...] = jnp.zeros_like(places_in)

    load_slots = load(places, slots, 7)
    load_slots.wait()
    load_up.wait()
    expand(wide, lambda s: up_v[1, s], slots, 0)
    load_inv.wait()

    def odd_product(cols):
        prod[:, cols] = mm(inv_v[...], wide[:, cols]).astype(BF16)

    column_blocks(odd_product)

    @pl.when(z < DEPTH - 1)
    def _():
        pl.semaphore_wait(near_sem, 1)

    @pl.when(z >= 2)
    def _():
        pl.semaphore_signal(far_sem, inc=1, device_id=up_line(-2), device_id_type=MESH)

    expand(even, lambda s: up_v[0, s], slots, 2)
    weight = (count + 2 * me).astype(F32) / count

    def up_product(cols):
        out = (-mm(even[...], prod[:, cols])).astype(BF16)
        new_up[:, cols] = out
        mean = jnp.sum(out.astype(F32), axis=0, keepdims=True) / P_SIZE
        term[:, cols] = weight * mean

    column_blocks(up_product)

    send_term = remote(term, pair_in, PAIR, PAIR, other_core)
    send_term.start()
    load_down.wait()
    expand(wide, lambda s: down_v[1, s], slots, 1)
    send_term.wait()
    pair[...] = term[...] + pair_in[...]
    sums[...] = term[...] + jnp.where(core == 1, pair_in[...], jnp.zeros_like(term))
    send_pair = [
        remote(pair, columns_in.at[j], COLUMN + j, COLUMN + j, device)
        for j, device in enumerate(same_z)
    ]
    for copy in send_pair:
        copy.start()
    column_blocks(odd_product)

    @pl.when(z < DEPTH - 2)
    def _():
        pl.semaphore_wait(far_sem, 1)

    load_diag.wait()
    expand(wide, lambda s: diag_v[s], slots, 4)

    def rest_product(cols):
        rest[:, cols] = wide[:, cols].astype(F32) - mm(even[...], prod[:, cols])

    column_blocks(rest_product)
    for copy in send_pair:
        copy.wait()
    lower = jnp.zeros_like(term)
    for j in range(columns - 1):
        got = columns_in[j]
        lower += jnp.where(column > j, got, jnp.zeros_like(got))
    sums[...] += lower
    rising[0] = lower + pair[...]
    falling[0] = lower

    def line_copies(n):
        up_step = remote(
            rising.at[n], rising_in.at[n], LINE + 2 * n, LINE + 2 * n, up_line(STEPS[n])
        )
        down_step = remote(
            falling.at[n],
            falling_in.at[n],
            LINE + 2 * n + 1,
            LINE + 2 * n + 1,
            up_line(-STEPS[n]),
        )
        return up_step, down_step

    def line_start(n):
        up_step, down_step = line_copies(n)

        @pl.when(z + STEPS[n] < DEPTH)
        def _():
            up_step.start()

        @pl.when(z >= STEPS[n])
        def _():
            down_step.start()

    def line_finish(n):
        up_step, down_step = line_copies(n)
        last = n == len(STEPS) - 1
        if not last:
            rising[n + 1] = rising[n]
            falling[n + 1] = falling[n]

        @pl.when(z >= STEPS[n])
        def _():
            down_step.wait_send()
            up_step.wait_recv()
            sums[...] += rising_in[n]
            if not last:
                rising[n + 1] += rising_in[n]

        @pl.when(z + STEPS[n] < DEPTH)
        def _():
            up_step.wait_send()
            down_step.wait_recv()
            sums[...] += falling_in[n]
            if not last:
                falling[n + 1] += falling_in[n]

    line_start(0)
    expand(even, lambda s: down_v[0, s], slots, 3)

    @pl.when(second)
    def _():
        for arrived, copy in zip(send_back, send_on):
            arrived.wait_recv()
            copy.start()

    line_finish(0)
    line_start(1)

    @pl.when(has_prev)
    def _():
        send_inv.wait_recv()

    def left_product(cols):
        left[:, cols] = mm(even[...], inv_in[:, cols]).astype(BF16)

    column_blocks(left_product)
    line_finish(1)
    line_start(2)

    @pl.when(has_prev)
    def _():
        send_up.wait_recv()
        send_places.wait_recv()

    load_slots_in = load(places_in, slots_in, 8)
    load_slots_in.wait()
    expand(wide, lambda s: up_in[s], slots_in, 0)

    def diag_product(cols):
        new_diag[:, cols] = (rest[:, cols] - mm(left[...], wide[:, cols])).astype(BF16)

    column_blocks(diag_product)

    @pl.when(third)
    def _():
        for arrived, copy in zip(send_back, send_home):
            arrived.wait_recv()
            copy.start()

    line_finish(2)

    @pl.when(has_prev)
    def _():
        send_down[0].wait_recv()

    expand(down_wide, lambda s: first_in[s], slots_in, 1, HALF)

    @pl.when(far_end | second | third)
    def _():
        for copy in send_back:
            copy.wait_send()

    @pl.when(has_next & ~far_end)
    def _():
        for copy in send_down:
            copy.wait_send()

    @pl.when(has_next)
    def _():
        send_inv.wait_send()
        send_up.wait_send()
        send_places.wait_send()

    @pl.when(has_prev)
    def _():
        send_down[1].wait_recv()


def exchange(sizes, *operands):
    dense = pltpu.VMEM((P_SIZE, P_SIZE), BF16)
    tiles = pltpu.VMEM((KT, TILE, TILE), BF16)
    half = pltpu.VMEM((HALF, TILE, TILE), BF16)
    row = pltpu.VMEM((1, P_SIZE), F32)
    rows = pltpu.VMEM((len(STEPS), 1, P_SIZE), F32)
    columns = sizes[0] * sizes[1] // (2 * DEPTH)
    return pl.pallas_call(
        functools.partial(exchange_kernel, sizes),
        name="exchange",
        out_shape=(
            dense,
            dense,
            half,
            pltpu.VMEM((NT, TILE), I32),
            dense,
            dense,
            row,
        ),
        in_specs=[pl.BlockSpec(memory_space=pltpu.HBM)] * 7,
        out_specs=(pl.BlockSpec(memory_space=pltpu.VMEM),) * 7,
        scratch_shapes=[
            pltpu.VMEM((2, KT), I32),
            pltpu.VMEM((2, KT), I32),
            pltpu.VMEM((1, KT), I32),
            pltpu.VMEM((2, KT, TILE, TILE), BF16),
            pltpu.VMEM((2, KT, TILE, TILE), BF16),
            tiles,
            dense,
            pltpu.VMEM((NT, TILE), I32),
            pltpu.SMEM((NT, TILE), I32),
            pltpu.SMEM((NT, TILE), I32),
            dense,
            tiles,
            half,
            tiles,
            dense,
            dense,
            dense,
            pltpu.VMEM((P_SIZE, P_SIZE), F32),
            row,
            row,
            row,
            pltpu.VMEM((columns - 1, 1, P_SIZE), F32),
            rows,
            rows,
            rows,
            rows,
            pltpu.SemaphoreType.DMA((9,)),
            pltpu.SemaphoreType.DMA((COLUMN + columns - 1,)),
            pltpu.SemaphoreType.DMA((COLUMN + columns - 1,)),
            pltpu.SemaphoreType.REGULAR,
            pltpu.SemaphoreType.REGULAR,
        ],
        compiler_params=pltpu.CompilerParams(
            collective_id=0, has_side_effects=True, vmem_limit_bytes=44 << 20
        ),
    )(*(pltpu.with_memory_space_constraint(x, pltpu.HBM) for x in operands))


def finish_kernel(
    places,
    left,
    wide_in,
    tiles,
    up_in,
    diag_in,
    sums_in,
    new_diag,
    new_up,
    new_down,
    sums,
    wide,
    out,
    sem,
):
    copies = [
        pltpu.make_async_copy(up_in, new_up.at[0], sem.at[0]),
        pltpu.make_async_copy(diag_in, new_diag.at[0], sem.at[1]),
    ]
    for copy in copies:
        copy.start()
    sums[...] = sums_in[...]
    for k in range(HALF, KT):
        p = jnp.clip(places[5, k], 0, NT * NT - 1)
        r = pl.multiple_of((p >> 3) * TILE, TILE)
        c = pl.multiple_of((p & 7) * TILE, TILE)
        wide[pl.ds(r, TILE), pl.ds(c, TILE)] = tiles[k - HALF]
    for b in range(P_SIZE // WIDE):
        rows = pl.ds(b * WIDE, WIDE)
        out[rows] = (-mm(left[rows], wide[...])).astype(BF16)
        copy = pltpu.make_async_copy(out.at[rows], new_down.at[0, rows], sem.at[2 + b])
        copy.start()
        copies.append(copy)
    for copy in copies:
        copy.wait()


def finish(places, left, wide, *operands):
    vmem = pl.BlockSpec(memory_space=pltpu.VMEM)
    hbm = pl.BlockSpec(memory_space=pltpu.HBM)
    square = jax.ShapeDtypeStruct((1, P_SIZE, P_SIZE), BF16)
    return pl.pallas_call(
        finish_kernel,
        name="finish",
        out_shape=(
            square,
            square,
            square,
            jax.ShapeDtypeStruct((1, P_SIZE), F32),
            pltpu.VMEM((P_SIZE, P_SIZE), BF16),
        ),
        in_specs=[pl.BlockSpec(memory_space=pltpu.SMEM)] + [vmem] * 6,
        out_specs=(hbm, hbm, hbm, vmem, vmem),
        scratch_shapes=[
            pltpu.VMEM((P_SIZE, P_SIZE), BF16),
            pltpu.SemaphoreType.DMA((2 + P_SIZE // WIDE,)),
        ],
        input_output_aliases={2: 4},
        compiler_params=pltpu.CompilerParams(vmem_limit_bytes=16 << 20),
    )(places, left, wide, *operands)


def local(sizes, up_tiles, up_at, down_tiles, down_at, diag_tiles, diag_at, odd_inverse):
    left, wide, down_in, places_in, new_up, new_diag, sums = exchange(
        sizes, up_at, down_at, diag_at, up_tiles, down_tiles, diag_tiles, odd_inverse
    )
    return finish(places_in, left, wide, down_in, new_up, new_diag, sums)[:4]


def solution(mesh):
    sizes = (mesh.shape["grp"], mesh.shape["lev"])
    return jax.shard_map(
        functools.partial(local, sizes),
        mesh=mesh,
        in_specs=(
            P(AXES, None, None, None),
            P(AXES, None),
            P(AXES, None, None, None),
            P(AXES, None),
            P(AXES, None, None, None),
            P(AXES, None),
            P(AXES, None, None),
        ),
        out_specs=(
            P(AXES, None, None),
            P(AXES, None, None),
            P(AXES, None, None),
            P(AXES, None),
        ),
        check_vma=False,
    )
```

time: 88.8 us -> 72.1 us (0.81)
  Pallas kernels: 80.1 us -> 71.4 us
  local copies, waits for them, and re-layouts: 7.25 us -> 0 us
    pallas_call x1, Pallas kernels: 74.8 us -> 66.9 us  [exchange(): pl.pallas_call(functools.partial(exchange_kernel, sizes), name='exchange'...]
    unnamed x12 -> x0, local copies, waits for them, and re-layouts: 7.25 us -> none
where the time goes in v3:
time: 72.1 us; the launch traced here: 72 us
  Pallas kernels  71.4 us (99%)
    pallas_call x1, Pallas kernels, exchange(): pl.pallas_call(functools.partial(exchange_kernel, sizes), name='exchange'...  66.9 us
    pallas_call x1, Pallas kernels, finish(): pl.pallas_call(finish_kernel, name='finish', out_shape=(square, square, s...  4.48 us

profile of v3, /device:TPU:8, one launch (start us, length us, event | category | flops | bytes accessed | tf_op | source)
XLA Modules:
  0.0 72.0 jit_solution(2713242515413727954)
XLA Ops:
  0.6 66.9 %exchange.1 = (bf16[1024,1024]{1,0:T(8,128)(2,1)S(1)}, bf16[1024,1024]{1,0:T(8,128)(2,1)S(1)}, bf16[12,128,128]{2,1,0:T(8,128)(2,1)S(1)}, s32[8,128]{1,0:T(8,128...) custom-call(s32[2,24]{1,0:T(2,128)} %up_at.1, s32[2,24]{1,0:T(2,128)} %down_at.1, ...), custom_call_target="tpu_custom_call" | custom-call | tf_op jit(solution)/shard_map/exchange/pallas_call | solution.py:443
  67.5 4.5 %finish.1 = (bf16[1,1024,1024]{2,1,0:T(8,128)(2,1)}, bf16[1,1024,1024]{2,1,0:T(8,128)(2,1)}, bf16[1,1024,1024]{2,1,0:T(8,128)(2,1)}, f32[1,1024]{1,0:T(1,128)}, bf16[1024,1024]{1,0:T(8,128)(2,1)S(1)}) custom-call(s32[8,128]{1,0:T(8,128)S(1)} %get-tuple-element.15.places, ...), custom_call_target="tpu_custom_call", output_to_operand_aliasing={{4}: (2, {})} | custom-call | tf_op jit(solution)/shard_map/finish/pallas_call | solution.py:538

commit v4 on v3

--- a/solution.py
+++ b/solution.py
@@ -21,22 +21,22 @@
 F32 = jnp.float32
 BF16 = jnp.bfloat16
 I32 = jnp.int32
-INV, UP, PLACE, DOWN, HOP, PAIR, LINE, COLUMN = 0, 1, 2, 3, 5, 7, 8, 14
+INV, UP, PLACE, DOWN, HOP, PAIR, RESULT, FIRST, LINE, COLUMN = 0, 2, 3, 4, 6, 7, 8, 9, 10, 16
 
 
 def mm(a, b):
     return jnp.dot(a, b, preferred_element_type=F32)
 
 
-def column_blocks(body):
+def column_blocks(body, wide=WIDE):
     def step(b, carry):
-        body(pl.ds(pl.multiple_of(b * WIDE, WIDE), WIDE))
+        body(pl.ds(pl.multiple_of(b * wide, wide), wide))
         return carry
 
-    lax.fori_loop(0, P_SIZE // WIDE, step, 0)
-
-
-def expand(dense, tile_of, slots, row, below=KT):
+    lax.fori_loop(0, P_SIZE // wide, step, 0)
+
+
+def expand(dense, tile_of, slots, row, below=KT, unroll=1):
     def tile_row(r, carry):
         rows = pl.ds(pl.multiple_of(r * TILE, TILE), TILE)
         for c in range(NT):
@@ -46,7 +46,7 @@
             dense[rows, c * TILE : (c + 1) * TILE] = jnp.where(here, tile, jnp.zeros_like(tile))
         return carry
 
-    lax.fori_loop(0, NT, tile_row, 0)
+    lax.fori_loop(0, NT, tile_row, 0, unroll=unroll)
 
 
 def slot_row(places):
@@ -97,6 +97,10 @@
     term,
     pair,
     pair_in,
+    before,
+    upto,
+    shared,
+    first_total,
     columns_in,
     rising,
     falling,
@@ -130,12 +134,15 @@
     ]
     has_next, has_prev = me < count - 1, me > 0
     inside = column < columns - 1
-    far_end = (core == 1) & (z == 7) & inside
-    second = (core == 1) & (z == 4) & inside
-    third = (core == 1) & (z == 1) & inside
-    hop_from = (core == 0) & (z == 0) & has_prev
+    first_core = core == 0
+    meets = first_core & (z >= 1)
+    giver = (core == 1) & (z == 7) & inside
+    far_end = first_core & (z == 7) & inside
+    second = first_core & (z == 4) & inside
+    third = first_core & (z == 1) & inside
+    hop_from = first_core & (z == 0) & has_prev
     target = place_of((column + 1) * 2 * DEPTH)
-    holder = place_of((column - 1) * 2 * DEPTH + 3)
+    holder = place_of((column - 1) * 2 * DEPTH + 2)
 
     def load(source, target, sem):
         copy = pltpu.make_async_copy(source, target, local_sem.at[sem])
@@ -154,13 +161,18 @@
 
     tell_if(has_prev, place_of(me - 1))
     tell(other_core)
-    tell_if(z >= 1, up_line(-1))
+    tell_if(first_core & (z >= 1), up_line(-1))
     for step in STEPS:
-        tell_if(z + step < DEPTH, up_line(step))
+        tell_if(first_core & (z + step < DEPTH), up_line(step))
     tell_if(second | third, up_line(3))
     tell_if(hop_from, holder)
-    for device in same_z:
-        tell(device)
+
+    tell_if(first_core & (z == 1), up_line(-1))
+
+    @pl.when(meets)
+    def _():
+        for device in same_z:
+            tell(device)
 
     load_up_at = load(up_at, up_at_v, 0)
     load_down_at = load(down_at, down_at_v, 1)
@@ -170,9 +182,11 @@
     load_down = load(down, down_v, 5)
     load_diag = load(diag.at[0], diag_v, 6)
 
-    expected = len(same_z) + 1
-    for condition in (has_next, z < DEPTH - 1, z >= 1, z >= 2, z >= 4, far_end, second, third):
-        expected += condition.astype(I32)
+    expected = 1 + has_next.astype(I32) + (far_end | second | third).astype(I32)
+    line = len(same_z) * (z >= 1).astype(I32)
+    for condition in (z == 0, z < DEPTH - 1, z >= 1, z >= 2, z >= 4):
+        line += condition.astype(I32)
+    expected += (1 - core) * line
     pl.semaphore_wait(barrier, expected)
 
     def remote(source, target, send, recv, device):
@@ -185,36 +199,36 @@
             device_id_type=MESH,
         )
 
+    following = place_of(me + 1)
     halves = [pl.ds(c * HALF, HALF) for c in range(2)]
-    following = place_of(me + 1)
-    send_inv = remote(inv.at[0], inv_in, INV, INV, following)
+    tall = [pl.ds(c * (P_SIZE // 2), P_SIZE // 2) for c in range(2)]
+    send_inv = [
+        remote(inv.at[0, rows], inv_in.at[rows], INV + c, INV + c, following)
+        for c, rows in enumerate(tall)
+    ]
     send_up = remote(up.at[1], up_in, UP, UP, following)
     send_places = remote(places, places_in, PLACE, PLACE, following)
     send_down = [
         remote(down.at[1, h], landing, DOWN + c, DOWN + c, following)
         for c, (h, landing) in enumerate(zip(halves, (first_in, down_in)))
     ]
-    send_back = [
-        remote(down.at[1, h], hop.at[h], HOP + c, HOP + c, up_line(-3))
-        for c, h in enumerate(halves)
-    ]
-    send_on = [
-        remote(hop.at[h], hop.at[h], HOP + c, HOP + c, up_line(-3)) for c, h in enumerate(halves)
-    ]
-    send_home = [
-        remote(hop.at[h], landing, HOP + c, DOWN + c, target)
-        for c, (h, landing) in enumerate(zip(halves, (first_in, down_in)))
-    ]
-
-    @pl.when(far_end)
-    def _():
-        for copy in send_back:
+    send_across = remote(down.at[1, halves[0]], hop, HOP, HOP, other_core)
+    send_back = remote(hop, hop, HOP, HOP, up_line(-3))
+    send_home = remote(hop, first_in, HOP, DOWN, target)
+
+    def forward(condition, copy):
+        @pl.when(condition)
+        def _():
+            send_across.wait_recv()
             copy.start()
 
+    @pl.when(giver)
+    def _():
+        send_across.start()
+
     @pl.when(has_next)
     def _():
-        send_inv.start()
-        send_up.start()
+        send_inv[0].start()
 
     load_up_at.wait()
     load_down_at.wait()
@@ -227,16 +241,7 @@
     places[4:5] = slot_row(diag_at_v[...])
     places[5:6, 0:KT] = down_at_v[1:2]
 
-    @pl.when(has_next)
-    def _():
-        send_places.start()
-
-    @pl.when(has_next & ~far_end)
-    def _():
-        for copy in send_down:
-            copy.start()
-
-    @pl.when(z >= 1)
+    @pl.when(first_core & (z >= 1))
     def _():
         pl.semaphore_signal(near_sem, inc=1, device_id=up_line(-1), device_id_type=MESH)
 
@@ -259,11 +264,13 @@
 
     column_blocks(odd_product)
 
-    @pl.when(z < DEPTH - 1)
+    forward(far_end, send_back)
+
+    @pl.when(first_core & (z < DEPTH - 1))
     def _():
         pl.semaphore_wait(near_sem, 1)
 
-    @pl.when(z >= 2)
+    @pl.when(first_core & (z >= 2))
     def _():
         pl.semaphore_signal(far_sem, inc=1, device_id=up_line(-2), device_id_type=MESH)
 
@@ -279,21 +286,56 @@
     column_blocks(up_product)
 
     send_term = remote(term, pair_in, PAIR, PAIR, other_core)
-    send_term.start()
+
+    @pl.when(~first_core)
+    def _():
+        send_term.start()
+
+    @pl.when(has_next)
+    def _():
+        send_inv[1].start()
+        send_places.start()
+        send_up.start()
+
+    @pl.when(has_next & ~giver)
+    def _():
+        send_down[0].start()
+
+    @pl.when(has_next)
+    def _():
+        send_down[1].start()
+
     load_down.wait()
     expand(wide, lambda s: down_v[1, s], slots, 1)
-    send_term.wait()
-    pair[...] = term[...] + pair_in[...]
-    sums[...] = term[...] + jnp.where(core == 1, pair_in[...], jnp.zeros_like(term))
     send_pair = [
-        remote(pair, columns_in.at[j], COLUMN + j, COLUMN + j, device)
+        remote(shared, columns_in.at[j], COLUMN + j, COLUMN + j, device)
         for j, device in enumerate(same_z)
     ]
-    for copy in send_pair:
-        copy.start()
     column_blocks(odd_product)
 
-    @pl.when(z < DEPTH - 2)
+    @pl.when(first_core)
+    def _():
+        send_term.wait_recv()
+        pair[...] = term[...] + pair_in[...]
+        shared[...] = pair[...]
+
+    send_first = remote(pair, first_total, FIRST, FIRST, up_line(1))
+
+    @pl.when(first_core & (z == 0))
+    def _():
+        send_first.start()
+
+    @pl.when(first_core & (z == 1))
+    def _():
+        send_first.wait_recv()
+        shared[...] += first_total[...]
+
+    @pl.when(meets)
+    def _():
+        for copy in send_pair:
+            copy.start()
+
+    @pl.when(first_core & (z < DEPTH - 2))
     def _():
         pl.semaphore_wait(far_sem, 1)
 
@@ -304,15 +346,26 @@
         rest[:, cols] = wide[:, cols].astype(F32) - mm(even[...], prod[:, cols])
 
     column_blocks(rest_product)
-    for copy in send_pair:
-        copy.wait()
-    lower = jnp.zeros_like(term)
-    for j in range(columns - 1):
-        got = columns_in[j]
-        lower += jnp.where(column > j, got, jnp.zeros_like(got))
-    sums[...] += lower
-    rising[0] = lower + pair[...]
-    falling[0] = lower
+    forward(second, send_back)
+
+    before[...] = jnp.zeros_like(before)
+
+    @pl.when(meets)
+    def _():
+        for copy in send_pair:
+            copy.wait()
+        for j in range(columns - 1):
+            got = columns_in[j]
+            before[...] += jnp.where(column > j, got, jnp.zeros_like(got))
+
+    @pl.when(first_core & (z == 0))
+    def _():
+        send_first.wait_send()
+
+    @pl.when(first_core)
+    def _():
+        rising[0] = before[...] + pair[...]
+        falling[0] = before[...]
 
     def line_copies(n):
         up_step = remote(
@@ -330,11 +383,11 @@
     def line_start(n):
         up_step, down_step = line_copies(n)
 
-        @pl.when(z + STEPS[n] < DEPTH)
+        @pl.when(first_core & (z + STEPS[n] < DEPTH))
         def _():
             up_step.start()
 
-        @pl.when(z >= STEPS[n])
+        @pl.when(first_core & (z >= STEPS[n]))
         def _():
             down_step.start()
 
@@ -345,88 +398,104 @@
             rising[n + 1] = rising[n]
             falling[n + 1] = falling[n]
 
-        @pl.when(z >= STEPS[n])
+        @pl.when(first_core & (z >= STEPS[n]))
         def _():
             down_step.wait_send()
             up_step.wait_recv()
-            sums[...] += rising_in[n]
+            before[...] += rising_in[n]
             if not last:
                 rising[n + 1] += rising_in[n]
 
-        @pl.when(z + STEPS[n] < DEPTH)
+        @pl.when(first_core & (z + STEPS[n] < DEPTH))
         def _():
             up_step.wait_send()
             down_step.wait_recv()
-            sums[...] += falling_in[n]
+            before[...] += falling_in[n]
             if not last:
                 falling[n + 1] += falling_in[n]
 
     line_start(0)
     expand(even, lambda s: down_v[0, s], slots, 3)
 
-    @pl.when(second)
-    def _():
-        for arrived, copy in zip(send_back, send_on):
-            arrived.wait_recv()
-            copy.start()
-
     line_finish(0)
     line_start(1)
 
     @pl.when(has_prev)
     def _():
-        send_inv.wait_recv()
+        for copy in send_inv:
+            copy.wait_recv()
 
     def left_product(cols):
         left[:, cols] = mm(even[...], inv_in[:, cols]).astype(BF16)
 
-    column_blocks(left_product)
+    column_blocks(left_product, 2 * WIDE)
     line_finish(1)
     line_start(2)
+    forward(third, send_home)
+    line_finish(2)
+    send_result = remote(upto, pair_in, RESULT, RESULT, other_core)
+
+    @pl.when(first_core)
+    def _():
+        upto[...] = before[...] + term[...]
+        sums[...] = upto[...]
+        send_result.start()
+
+
+    def lay_first_half():
+        send_down[0].wait_recv()
+        expand(down_wide, lambda s: first_in[s], slots_in, 1, HALF, unroll=True)
 
     @pl.when(has_prev)
     def _():
-        send_up.wait_recv()
         send_places.wait_recv()
 
     load_slots_in = load(places_in, slots_in, 8)
     load_slots_in.wait()
-    expand(wide, lambda s: up_in[s], slots_in, 0)
+    pl.when(hop_from)(lay_first_half)
+
+    @pl.when(has_prev)
+    def _():
+        send_up.wait_recv()
+
+    expand(wide, lambda s: up_in[s], slots_in, 0, unroll=True)
 
     def diag_product(cols):
         new_diag[:, cols] = (rest[:, cols] - mm(left[...], wide[:, cols])).astype(BF16)
 
-    column_blocks(diag_product)
-
-    @pl.when(third)
-    def _():
-        for arrived, copy in zip(send_back, send_home):
-            arrived.wait_recv()
-            copy.start()
-
-    line_finish(2)
-
-    @pl.when(has_prev)
-    def _():
-        send_down[0].wait_recv()
-
-    expand(down_wide, lambda s: first_in[s], slots_in, 1, HALF)
-
-    @pl.when(far_end | second | third)
-    def _():
-        for copy in send_back:
+    column_blocks(diag_product, 2 * WIDE)
+
+    pl.when(has_prev & ~hop_from)(lay_first_half)
+
+    @pl.when(me == 0)
+    def _():
+        down_wide[...] = jnp.zeros_like(down_wide)
+
+    @pl.when(giver | far_end | second | third)
+    def _():
+        send_back.wait_send()
+
+    @pl.when(has_next & ~giver)
+    def _():
+        send_down[0].wait_send()
+
+    @pl.when(has_next)
+    def _():
+        for copy in send_inv:
             copy.wait_send()
-
-    @pl.when(has_next & ~far_end)
-    def _():
-        for copy in send_down:
-            copy.wait_send()
-
-    @pl.when(has_next)
-    def _():
-        send_inv.wait_send()
         send_up.wait_send()
         send_places.wait_send()
+        send_down[1].wait_send()
+
+    @pl.when(first_core)
+    def _():
+        send_result.wait_send()
+
+    @pl.when(~first_core)
+    def _():
+        send_term.wait_send()
+        send_result.wait_recv()
+        sums[...] = term[...] + pair_in[...]
 
     @pl.when(has_prev)
     def _():
@@ -468,11 +537,15 @@
             dense,
             tiles,
             half,
-            tiles,
+            half,
             dense,
             dense,
             dense,
             pltpu.VMEM((P_SIZE, P_SIZE), F32),
+            row,
+            row,
+            row,
+            row,
             row,
             row,
             row,

time: 72.1 us -> 59 us (0.82)
  Pallas kernels: 71.4 us -> 58.3 us
    pallas_call x1, Pallas kernels: 66.9 us -> 53.8 us  [exchange(): pl.pallas_call(functools.partial(exchange_kernel, sizes), name='exchange'...]
where the time goes in v4:
time: 59 us; the launch traced here: 58.9 us
  Pallas kernels  58.3 us (99%)
  between operations  0.64 us (1%)
    pallas_call x1, Pallas kernels, exchange(): pl.pallas_call(functools.partial(exchange_kernel, sizes), name='exchange'...  53.8 us
    pallas_call x1, Pallas kernels, finish(): pl.pallas_call(finish_kernel, name='finish', out_shape=(square, square, s...  4.49 us

profile of v4, /device:TPU:8, one launch (start us, length us, event | category | flops | bytes accessed | tf_op | source)
XLA Modules:
  0.0 58.9 jit_solution(14828315167749929010)
XLA Ops:
  0.6 53.8 %exchange.1 = (bf16[1024,1024]{1,0:T(8,128)(2,1)S(1)}, bf16[1024,1024]{1,0:T(8,128)(2,1)S(1)}, bf16[12,128,128]{2,1,0:T(8,128)(2,1)S(1)}, s32[8,128]{1,0:T(8,128...) custom-call(s32[2,24]{1,0:T(2,128)} %up_at.1, s32[2,24]{1,0:T(2,128)} %down_at.1, ...), custom_call_target="tpu_custom_call" | custom-call | tf_op jit(solution)/shard_map/exchange/pallas_call | solution.py:512
  54.4 4.5 %finish.1 = (bf16[1,1024,1024]{2,1,0:T(8,128)(2,1)}, bf16[1,1024,1024]{2,1,0:T(8,128)(2,1)}, bf16[1,1024,1024]{2,1,0:T(8,128)(2,1)}, f32[1,1024]{1,0:T(1,128)}, bf16[1024,1024]{1,0:T(8,128)(2,1)S(1)}) custom-call(s32[8,128]{1,0:T(8,128)S(1)} %get-tuple-element.15.places, ...), custom_call_target="tpu_custom_call", output_to_operand_aliasing={{4}: (2, {})} | custom-call | tf_op jit(solution)/shard_map/finish/pallas_call | solution.py:611

commit v5 on v4

--- a/solution.py
+++ b/solution.py
@@ -138,11 +138,11 @@
     meets = first_core & (z >= 1)
     giver = (core == 1) & (z == 7) & inside
     far_end = first_core & (z == 7) & inside
-    second = first_core & (z == 4) & inside
-    third = first_core & (z == 1) & inside
+    second = first_core & (z == 4) & (column >= 1)
+    third = first_core & (z == 1) & (column >= 1)
     hop_from = first_core & (z == 0) & has_prev
-    target = place_of((column + 1) * 2 * DEPTH)
-    holder = place_of((column - 1) * 2 * DEPTH + 2)
+    middle = place_of((column + 1) * 2 * DEPTH + 8)
+    giving = place_of((column - 1) * 2 * DEPTH + 14)
 
     def load(source, target, sem):
         copy = pltpu.make_async_copy(source, target, local_sem.at[sem])
@@ -164,8 +164,8 @@
     tell_if(first_core & (z >= 1), up_line(-1))
     for step in STEPS:
         tell_if(first_core & (z + step < DEPTH), up_line(step))
-    tell_if(second | third, up_line(3))
-    tell_if(hop_from, holder)
+    tell_if(third, up_line(3))
+    tell_if(second, giving)
 
     tell_if(first_core & (z == 1), up_line(-1))
 
@@ -182,7 +182,7 @@
     load_down = load(down, down_v, 5)
     load_diag = load(diag.at[0], diag_v, 6)
 
-    expected = 1 + has_next.astype(I32) + (far_end | second | third).astype(I32)
+    expected = 1 + has_next.astype(I32) + (far_end | second).astype(I32)
     line = len(same_z) * (z >= 1).astype(I32)
     for condition in (z == 0, z < DEPTH - 1, z >= 1, z >= 2, z >= 4):
         line += condition.astype(I32)
@@ -213,8 +213,9 @@
         for c, (h, landing) in enumerate(zip(halves, (first_in, down_in)))
     ]
     send_across = remote(down.at[1, halves[0]], hop, HOP, HOP, other_core)
+    send_over = remote(hop, hop, HOP, HOP, middle)
     send_back = remote(hop, hop, HOP, HOP, up_line(-3))
-    send_home = remote(hop, first_in, HOP, DOWN, target)
+    send_home = remote(hop, first_in, HOP, DOWN, up_line(-1))
 
     def forward(condition, copy):
         @pl.when(condition)
@@ -257,14 +258,13 @@
     load_slots.wait()
     load_up.wait()
     expand(wide, lambda s: up_v[1, s], slots, 0)
+    forward(far_end, send_over)
     load_inv.wait()
 
     def odd_product(cols):
         prod[:, cols] = mm(inv_v[...], wide[:, cols]).astype(BF16)
 
     column_blocks(odd_product)
-
-    forward(far_end, send_back)
 
     @pl.when(first_core & (z < DEPTH - 1))
     def _():
@@ -429,9 +429,9 @@
         left[:, cols] = mm(even[...], inv_in[:, cols]).astype(BF16)
 
     column_blocks(left_product, 2 * WIDE)
+    forward(third, send_home)
     line_finish(1)
     line_start(2)
-    forward(third, send_home)
     line_finish(2)
     send_result = remote(upto, pair_in, RESULT, RESULT, other_core)
 

time: 59 us -> 51.3 us (0.87)
  Pallas kernels: 58.3 us -> 50.2 us
    pallas_call x1, Pallas kernels: 53.8 us -> 45.7 us  [exchange(): pl.pallas_call(functools.partial(exchange_kernel, sizes), name='exchange'...]
where the time goes in v5:
time: 51.3 us; the launch traced here: 50.9 us
  Pallas kernels  50.2 us (98%)
  between operations  0.64 us (1%)
    pallas_call x1, Pallas kernels, exchange(): pl.pallas_call(functools.partial(exchange_kernel, sizes), name='exchange'...  45.7 us
    pallas_call x1, Pallas kernels, finish(): pl.pallas_call(finish_kernel, name='finish', out_shape=(square, square, s...  4.49 us

profile of v5, /device:TPU:8, one launch (start us, length us, event | category | flops | bytes accessed | tf_op | source)
XLA Modules:
  0.0 50.9 jit_solution(13449398751248298357)
XLA Ops:
  0.6 45.7 %exchange.1 = (bf16[1024,1024]{1,0:T(8,128)(2,1)S(1)}, bf16[1024,1024]{1,0:T(8,128)(2,1)S(1)}, bf16[12,128,128]{2,1,0:T(8,128)(2,1)S(1)}, s32[8,128]{1,0:T(8,128...) custom-call(s32[2,24]{1,0:T(2,128)} %up_at.1, s32[2,24]{1,0:T(2,128)} %down_at.1, ...), custom_call_target="tpu_custom_call" | custom-call | tf_op jit(solution)/shard_map/exchange/pallas_call | solution.py:512
  46.4 4.5 %finish.1 = (bf16[1,1024,1024]{2,1,0:T(8,128)(2,1)}, bf16[1,1024,1024]{2,1,0:T(8,128)(2,1)}, bf16[1,1024,1024]{2,1,0:T(8,128)(2,1)}, f32[1,1024]{1,0:T(1,128)}, bf16[1024,1024]{1,0:T(8,128)(2,1)S(1)}) custom-call(s32[8,128]{1,0:T(8,128)S(1)} %get-tuple-element.15.places, ...), custom_call_target="tpu_custom_call", output_to_operand_aliasing={{4}: (2, {})} | custom-call | tf_op jit(solution)/shard_map/finish/pallas_call | solution.py:611

commit v6 on v5

--- a/solution.py
+++ b/solution.py
@@ -11,7 +11,7 @@
 NT = 8
 P_SIZE = 1024
 KT = 24
-HALF = KT // 2
+FIRST_TILES = 14
 WIDE = 256
 DEPTH = 8
 SIDE = 4
@@ -21,7 +21,7 @@
 F32 = jnp.float32
 BF16 = jnp.bfloat16
 I32 = jnp.int32
-INV, UP, PLACE, DOWN, HOP, PAIR, RESULT, FIRST, LINE, COLUMN = 0, 2, 3, 4, 6, 7, 8, 9, 10, 16
+INV, UP, PLACE, DOWN, HOP, HOME, PAIR, RESULT, FIRST, LINE, COLUMN = 0, 2, 3, 4, 6, 8, 10, 11, 12, 13, 19
 
 
 def mm(a, b):
@@ -72,7 +72,7 @@
     left,
     down_wide,
     down_in,
-    places_in,
+    slots_in,
     new_up,
     new_diag,
     sums,
@@ -85,7 +85,7 @@
     inv_v,
     places,
     slots,
-    slots_in,
+    places_in,
     inv_in,
     up_in,
     first_in,
@@ -200,7 +200,7 @@
         )
 
     following = place_of(me + 1)
-    halves = [pl.ds(c * HALF, HALF) for c in range(2)]
+    halves = [pl.ds(0, FIRST_TILES), pl.ds(FIRST_TILES, KT - FIRST_TILES)]
     tall = [pl.ds(c * (P_SIZE // 2), P_SIZE // 2) for c in range(2)]
     send_inv = [
         remote(inv.at[0, rows], inv_in.at[rows], INV + c, INV + c, following)
@@ -212,20 +212,32 @@
         remote(down.at[1, h], landing, DOWN + c, DOWN + c, following)
         for c, (h, landing) in enumerate(zip(halves, (first_in, down_in)))
     ]
-    send_across = remote(down.at[1, halves[0]], hop, HOP, HOP, other_core)
-    send_over = remote(hop, hop, HOP, HOP, middle)
-    send_back = remote(hop, hop, HOP, HOP, up_line(-3))
-    send_home = remote(hop, first_in, HOP, DOWN, up_line(-1))
-
-    def forward(condition, copy):
+    pieces = [pl.ds(p * (FIRST_TILES // 2), FIRST_TILES // 2) for p in range(2)]
+    send_across = [
+        remote(down.at[1, r], hop.at[r], HOP + p, HOP + p, other_core) for p, r in enumerate(pieces)
+    ]
+    send_over = [
+        remote(hop.at[r], hop.at[r], HOP + p, HOP + p, middle) for p, r in enumerate(pieces)
+    ]
+    send_back = [
+        remote(hop.at[r], hop.at[r], HOP + p, HOP + p, up_line(-3)) for p, r in enumerate(pieces)
+    ]
+    send_home = [
+        remote(hop.at[r], first_in.at[r], HOP + p, HOME + p, up_line(-1))
+        for p, r in enumerate(pieces)
+    ]
+
+    def forward(condition, copies):
         @pl.when(condition)
         def _():
-            send_across.wait_recv()
+            for arriving, copy in zip(send_across, copies):
+                arriving.wait_recv()
+                copy.start()
+
+    @pl.when(giver)
+    def _():
+        for copy in send_across:
             copy.start()
-
-    @pl.when(giver)
-    def _():
-        send_across.start()
 
     @pl.when(has_next)
     def _():
@@ -442,9 +454,10 @@
         send_result.start()
 
 
-    def lay_first_half():
-        send_down[0].wait_recv()
-        expand(down_wide, lambda s: first_in[s], slots_in, 1, HALF, unroll=True)
+    def lay_first(copies):
+        for copy in copies:
+            copy.wait_recv()
+        expand(down_wide, lambda s: first_in[s], slots_in, 1, FIRST_TILES, unroll=True)
 
     @pl.when(has_prev)
     def _():
@@ -452,7 +465,7 @@
 
     load_slots_in = load(places_in, slots_in, 8)
     load_slots_in.wait()
-    pl.when(hop_from)(lay_first_half)
+    pl.when(hop_from)(functools.partial(lay_first, send_home))
 
     @pl.when(has_prev)
     def _():
@@ -465,7 +478,7 @@
 
     column_blocks(diag_product, 2 * WIDE)
 
-    pl.when(has_prev & ~hop_from)(lay_first_half)
+    pl.when(has_prev & ~hop_from)(functools.partial(lay_first, send_down[:1]))
 
     @pl.when(me == 0)
     def _():
@@ -473,7 +486,8 @@
 
     @pl.when(giver | far_end | second | third)
     def _():
-        send_back.wait_send()
+        for copy in send_back:
+            copy.wait_send()
 
     @pl.when(has_next & ~giver)
     def _():
@@ -505,7 +519,8 @@
 def exchange(sizes, *operands):
     dense = pltpu.VMEM((P_SIZE, P_SIZE), BF16)
     tiles = pltpu.VMEM((KT, TILE, TILE), BF16)
-    half = pltpu.VMEM((HALF, TILE, TILE), BF16)
+    half = pltpu.VMEM((FIRST_TILES, TILE, TILE), BF16)
+    others = pltpu.VMEM((KT - FIRST_TILES, TILE, TILE), BF16)
     row = pltpu.VMEM((1, P_SIZE), F32)
     rows = pltpu.VMEM((len(STEPS), 1, P_SIZE), F32)
     columns = sizes[0] * sizes[1] // (2 * DEPTH)
@@ -515,14 +530,16 @@
         out_shape=(
             dense,
             dense,
-            half,
-            pltpu.VMEM((NT, TILE), I32),
+            others,
+            pltpu.SMEM((NT, TILE), I32),
             dense,
             dense,
             row,
         ),
         in_specs=[pl.BlockSpec(memory_space=pltpu.HBM)] * 7,
-        out_specs=(pl.BlockSpec(memory_space=pltpu.VMEM),) * 7,
+        out_specs=(pl.BlockSpec(memory_space=pltpu.VMEM),) * 3
+        + (pl.BlockSpec(memory_space=pltpu.SMEM),)
+        + (pl.BlockSpec(memory_space=pltpu.VMEM),) * 3,
         scratch_shapes=[
             pltpu.VMEM((2, KT), I32),
             pltpu.VMEM((2, KT), I32),
@@ -533,7 +550,7 @@
             dense,
             pltpu.VMEM((NT, TILE), I32),
             pltpu.SMEM((NT, TILE), I32),
-            pltpu.SMEM((NT, TILE), I32),
+            pltpu.VMEM((NT, TILE), I32),
             dense,
             tiles,
             half,
@@ -586,14 +603,14 @@
         pltpu.make_async_copy(up_in, new_up.at[0], sem.at[0]),
         pltpu.make_async_copy(diag_in, new_diag.at[0], sem.at[1]),
     ]
+    copies.append(pltpu.make_async_copy(sums_in, sums, sem.at[6]))
     for copy in copies:
         copy.start()
-    sums[...] = sums_in[...]
-    for k in range(HALF, KT):
+    for k in range(FIRST_TILES, KT):
         p = jnp.clip(places[5, k], 0, NT * NT - 1)
         r = pl.multiple_of((p >> 3) * TILE, TILE)
         c = pl.multiple_of((p & 7) * TILE, TILE)
-        wide[pl.ds(r, TILE), pl.ds(c, TILE)] = tiles[k - HALF]
+        wide[pl.ds(r, TILE), pl.ds(c, TILE)] = tiles[k - FIRST_TILES]
     for b in range(P_SIZE // WIDE):
         rows = pl.ds(b * WIDE, WIDE)
         out[rows] = (-mm(left[rows], wide[...])).astype(BF16)
@@ -619,10 +636,10 @@
             pltpu.VMEM((P_SIZE, P_SIZE), BF16),
         ),
         in_specs=[pl.BlockSpec(memory_space=pltpu.SMEM)] + [vmem] * 6,
-        out_specs=(hbm, hbm, hbm, vmem, vmem),
+        out_specs=(hbm, hbm, hbm, hbm, vmem),
         scratch_shapes=[
             pltpu.VMEM((P_SIZE, P_SIZE), BF16),
-            pltpu.SemaphoreType.DMA((2 + P_SIZE // WIDE,)),
+            pltpu.SemaphoreType.DMA((3 + P_SIZE // WIDE,)),
         ],
         input_output_aliases={2: 4},
         compiler_params=pltpu.CompilerParams(vmem_limit_bytes=16 << 20),

time: 51.3 us -> 49.6 us (0.967)
  Pallas kernels: 50.2 us -> 48.4 us
    pallas_call x1, Pallas kernels: 4.49 us -> 3.29 us  [finish(): pl.pallas_call(finish_kernel, name='finish', out_shape=(square, square, s...]
    pallas_call x1, Pallas kernels: 45.7 us -> 45.1 us  [exchange(): pl.pallas_call(functools.partial(exchange_kernel, sizes), name='exchange'...]
where the time goes in v6:
time: 49.6 us; the launch traced here: 49 us
  Pallas kernels  48.4 us (98%)
  between operations  0.64 us (1%)
    pallas_call x1, Pallas kernels, exchange(): pl.pallas_call(functools.partial(exchange_kernel, sizes), name='exchange'...  45.1 us
    pallas_call x1, Pallas kernels, finish(): pl.pallas_call(finish_kernel, name='finish', out_shape=(square, square, s...  3.29 us

profile of v6, /device:TPU:8, one launch (start us, length us, event | category | flops | bytes accessed | tf_op | source)
XLA Modules:
  0.0 49.0 jit_solution(16454127610019012680)
XLA Ops:
  0.6 45.1 %exchange.1 = (bf16[1024,1024]{1,0:T(8,128)(2,1)S(1)}, bf16[1024,1024]{1,0:T(8,128)(2,1)S(1)}, bf16[10,128,128]{2,1,0:T(8,128)(2,1)S(1)}, s32[8,128]{1,0:T(8,128...) custom-call(s32[2,24]{1,0:T(2,128)} %up_at.1, s32[2,24]{1,0:T(2,128)} %down_at.1, ...), custom_call_target="tpu_custom_call" | custom-call | tf_op jit(solution)/shard_map/exchange/pallas_call | solution.py:527
  45.7 3.3 %finish.1 = (bf16[1,1024,1024]{2,1,0:T(8,128)(2,1)}, bf16[1,1024,1024]{2,1,0:T(8,128)(2,1)}, bf16[1,1024,1024]{2,1,0:T(8,128)(2,1)}, f32[1,1024]{1,0:T(1,128)}, bf16[1024,1024]{1,0:T(8,128)(2,1)S(1)}) custom-call(s32[8,128]{1,0:T(8,128)S(4)} %get-tuple-element.15.places, ...), custom_call_target="tpu_custom_call", output_to_operand_aliasing={{4}: (2, {})} | custom-call | tf_op jit(solution)/shard_map/finish/pallas_call | solution.py:628

commit v7 on v6

--- a/solution.py
+++ b/solution.py
@@ -11,8 +11,9 @@
 NT = 8
 P_SIZE = 1024
 KT = 24
-FIRST_TILES = 14
+FIRST_TILES = 16
 WIDE = 256
+HEIGHTS = (256, 256, 256, 128, 128)
 DEPTH = 8
 SIDE = 4
 STEPS = (1, 2, 4)
@@ -227,12 +228,12 @@
         for p, r in enumerate(pieces)
     ]
 
-    def forward(condition, copies):
+    def forward(condition, copies, which=(0, 1)):
         @pl.when(condition)
         def _():
-            for arriving, copy in zip(send_across, copies):
-                arriving.wait_recv()
-                copy.start()
+            for p in which:
+                send_across[p].wait_recv()
+                copies[p].start()
 
     @pl.when(giver)
     def _():
@@ -267,10 +268,10 @@
         places_in[...] = jnp.zeros_like(places_in)
 
     load_slots = load(places, slots, 7)
+    forward(far_end, send_over)
     load_slots.wait()
     load_up.wait()
     expand(wide, lambda s: up_v[1, s], slots, 0)
-    forward(far_end, send_over)
     load_inv.wait()
 
     def odd_product(cols):
@@ -357,8 +358,9 @@
     def rest_product(cols):
         rest[:, cols] = wide[:, cols].astype(F32) - mm(even[...], prod[:, cols])
 
+    forward(second, send_back, (0,))
     column_blocks(rest_product)
-    forward(second, send_back)
+    forward(second, send_back, (1,))
 
     before[...] = jnp.zeros_like(before)
 
@@ -431,6 +433,7 @@
 
     line_finish(0)
     line_start(1)
+    forward(third, send_home, (0,))
 
     @pl.when(has_prev)
     def _():
@@ -441,7 +444,7 @@
         left[:, cols] = mm(even[...], inv_in[:, cols]).astype(BF16)
 
     column_blocks(left_product, 2 * WIDE)
-    forward(third, send_home)
+    forward(third, send_home, (1,))
     line_finish(1)
     line_start(2)
     line_finish(2)
@@ -603,7 +606,7 @@
         pltpu.make_async_copy(up_in, new_up.at[0], sem.at[0]),
         pltpu.make_async_copy(diag_in, new_diag.at[0], sem.at[1]),
     ]
-    copies.append(pltpu.make_async_copy(sums_in, sums, sem.at[6]))
+    copies.append(pltpu.make_async_copy(sums_in, sums, sem.at[2]))
     for copy in copies:
         copy.start()
     for k in range(FIRST_TILES, KT):
@@ -611,12 +614,14 @@
         r = pl.multiple_of((p >> 3) * TILE, TILE)
         c = pl.multiple_of((p & 7) * TILE, TILE)
         wide[pl.ds(r, TILE), pl.ds(c, TILE)] = tiles[k - FIRST_TILES]
-    for b in range(P_SIZE // WIDE):
-        rows = pl.ds(b * WIDE, WIDE)
+    start = 0
+    for b, height in enumerate(HEIGHTS):
+        rows = pl.ds(start, height)
         out[rows] = (-mm(left[rows], wide[...])).astype(BF16)
-        copy = pltpu.make_async_copy(out.at[rows], new_down.at[0, rows], sem.at[2 + b])
+        copy = pltpu.make_async_copy(out.at[rows], new_down.at[0, rows], sem.at[3 + b])
         copy.start()
         copies.append(copy)
+        start += height
     for copy in copies:
         copy.wait()
 
@@ -639,7 +644,7 @@
         out_specs=(hbm, hbm, hbm, hbm, vmem),
         scratch_shapes=[
             pltpu.VMEM((P_SIZE, P_SIZE), BF16),
-            pltpu.SemaphoreType.DMA((3 + P_SIZE // WIDE,)),
+            pltpu.SemaphoreType.DMA((3 + len(HEIGHTS),)),
         ],
         input_output_aliases={2: 4},
         compiler_params=pltpu.CompilerParams(vmem_limit_bytes=16 << 20),

time: 49.6 us -> 49 us (0.988)
  no operation moved by 1% of the time
where the time goes in v7:
time: 49 us; the launch traced here: 48.6 us
  Pallas kernels  48 us (98%)
  between operations  0.64 us (1%)
    pallas_call x1, Pallas kernels, exchange(): pl.pallas_call(functools.partial(exchange_kernel, sizes), name='exchange'...  44.8 us
    pallas_call x1, Pallas kernels, finish(): pl.pallas_call(finish_kernel, name='finish', out_shape=(square, square, s...  3.19 us

profile of v7, /device:TPU:8, one launch (start us, length us, event | category | flops | bytes accessed | tf_op | source)
XLA Modules:
  0.0 48.6 jit_solution(3679213500087095833)
XLA Ops:
  0.6 44.8 %exchange.1 = (bf16[1024,1024]{1,0:T(8,128)(2,1)S(1)}, bf16[1024,1024]{1,0:T(8,128)(2,1)S(1)}, bf16[8,128,128]{2,1,0:T(8,128)(2,1)S(1)}, s32[8,128]{1,0:T(8,128)...) custom-call(s32[2,24]{1,0:T(2,128)} %up_at.1, s32[2,24]{1,0:T(2,128)} %down_at.1, ...), custom_call_target="tpu_custom_call" | custom-call | tf_op jit(solution)/shard_map/exchange/pallas_call | solution.py:530
  45.4 3.2 %finish.1 = (bf16[1,1024,1024]{2,1,0:T(8,128)(2,1)}, bf16[1,1024,1024]{2,1,0:T(8,128)(2,1)}, bf16[1,1024,1024]{2,1,0:T(8,128)(2,1)}, f32[1,1024]{1,0:T(1,128)}, bf16[1024,1024]{1,0:T(8,128)(2,1)S(1)}) custom-call(s32[8,128]{1,0:T(8,128)S(4)} %get-tuple-element.15.places, ...), custom_call_target="tpu_custom_call", output_to_operand_aliasing={{4}: (2, {})} | custom-call | tf_op jit(solution)/shard_map/finish/pallas_call | solution.py:633

commit v8 on v7

--- a/solution.py
+++ b/solution.py
@@ -180,8 +180,6 @@
     load_diag_at = load(diag_at, diag_at_v, 2)
     load_up = load(up, up_v, 3)
     load_inv = load(inv.at[0], inv_v, 4)
-    load_down = load(down, down_v, 5)
-    load_diag = load(diag.at[0], diag_v, 6)
 
     expected = 1 + has_next.astype(I32) + (far_end | second).astype(I32)
     line = len(same_z) * (z >= 1).astype(I32)
@@ -244,6 +242,8 @@
     def _():
         send_inv[0].start()
 
+    load_down = load(down, down_v, 5)
+    load_diag = load(diag.at[0], diag_v, 6)
     load_up_at.wait()
     load_down_at.wait()
     load_diag_at.wait()

time: 49 us -> 49 us (level)
  no operation moved by 1% of the time
where the time goes in v8:
time: 49 us; the launch traced here: 48.6 us
  Pallas kernels  48 us (98%)
  between operations  0.64 us (1%)
    pallas_call x1, Pallas kernels, exchange(): pl.pallas_call(functools.partial(exchange_kernel, sizes), name='exchange'...  44.8 us
    pallas_call x1, Pallas kernels, finish(): pl.pallas_call(finish_kernel, name='finish', out_shape=(square, square, s...  3.19 us

profile of v8, /device:TPU:8, one launch (start us, length us, event | category | flops | bytes accessed | tf_op | source)
XLA Modules:
  0.0 48.6 jit_solution(12837793646034623323)
XLA Ops:
  0.6 44.8 %exchange.1 = (bf16[1024,1024]{1,0:T(8,128)(2,1)S(1)}, bf16[1024,1024]{1,0:T(8,128)(2,1)S(1)}, bf16[8,128,128]{2,1,0:T(8,128)(2,1)S(1)}, s32[8,128]{1,0:T(8,128)...) custom-call(s32[2,24]{1,0:T(2,128)} %up_at.1, s32[2,24]{1,0:T(2,128)} %down_at.1, ...), custom_call_target="tpu_custom_call" | custom-call | tf_op jit(solution)/shard_map/exchange/pallas_call | solution.py:530
  45.4 3.2 %finish.1 = (bf16[1,1024,1024]{2,1,0:T(8,128)(2,1)}, bf16[1,1024,1024]{2,1,0:T(8,128)(2,1)}, bf16[1,1024,1024]{2,1,0:T(8,128)(2,1)}, f32[1,1024]{1,0:T(1,128)}, bf16[1024,1024]{1,0:T(8,128)(2,1)S(1)}) custom-call(s32[8,128]{1,0:T(8,128)S(4)} %get-tuple-element.15.places, ...), custom_call_target="tpu_custom_call", output_to_operand_aliasing={{4}: (2, {})} | custom-call | tf_op jit(solution)/shard_map/finish/pallas_call | solution.py:633
